TPU v7x, 128 devices: a whole 4x4x4 slice. The times are simulated.
128 devices in a mesh: cuts: 2 (over x_hi), section: 4 (over y), dp: 16 (over z, x_lo, core).
Axes of the slice: x: 4 (x_hi: 2, x_lo: 2; x = x_hi * 2 + x_lo), y: 4, z: 4, core: 2. Of those that a mesh axis runs over, the one named last changes fastest.
Arguments:
- activations: bfloat16 [2, 4, 4096, 4096], P('cuts', 'section', 'dp'), may hold values from -6 to 6
- upstream_grad: bfloat16 [2, 4, 4096, 4096], P('cuts', 'section', 'dp'), may hold values from -6 to 6
- routes: int32 [2, 4, 4096, 4], P('cuts', 'section', 'dp'), may hold values from 0 to 15, as said below
- router_probs: float32 [2, 4, 4096, 4], P('cuts', 'section', 'dp'), may hold values from 0.2 to 1
- gate_weight: bfloat16 [4, 5376, 4096], P('section', 'dp'), may hold values from -0.09375 to 0.09375
- up_weight: bfloat16 [4, 5376, 4096], P('section', 'dp'), may hold values from -0.09375 to 0.09375
- down_weight: bfloat16 [4, 5376, 4096], P('section', 'dp'), may hold values from -0.078125 to 0.078125
Outputs:
- grad_gate: bfloat16 [4, 5376, 4096], P('section', 'dp')
- grad_up: bfloat16 [4, 5376, 4096], P('section', 'dp')
- grad_down: bfloat16 [4, 5376, 4096], P('section', 'dp')
- prev_grad: bfloat16 [2, 4, 4096, 4096], P('cuts', 'section', 'dp')
Inputs may be any that keep to these rules, and one draw needn't show every extreme that they name: `routes`: each token names 4 different experts. In every aligned block of 256 tokens of one replica and section, from 32 to 64 tokens name expert 0, and in every draw some block has exactly 64.
All inputs are finite; a program needn't handle non-finite values.
Results may differ from a plain program's by a relative error of at most 0.025.
Values may be sent and summed in bfloat16 or wider, within the bound.
No kernel may reach another device: no remote copies, remote signals or barrier semaphores. Data moves between devices by JAX's collectives and lax.ppermute only.
A program may use at most 192 MiB of HBM per device.

v0:
```python
import jax
import jax.numpy as jnp
from jax import lax
from jax.experimental import pallas as pl
from jax.experimental.pallas import tpu as pltpu
from jax.sharding import PartitionSpec as P

CAP = 64
AXES = ("cuts", "dp")


def place(x, z, core):
    return (x // 2) * 16 + z * 4 + (x % 2) * 2 + core


def route(fx, fz, fc):
    return [
        (place(x, z, c), place(fx(x) % 4, fz(z) % 4, fc(c)))
        for x in range(4)
        for z in range(4)
        for c in range(2)
    ]


def keep(v):
    return v


INNER = route(lambda x: x ^ 1, keep, keep)
OUTER = route(lambda x: 3 - x, keep, keep)
UP = route(keep, lambda z: z + 1, keep)
DOWN = route(keep, lambda z: z - 1, keep)
ACROSS = route(keep, lambda z: z + 2, keep)
SIBLING = route(keep, keep, lambda c: 1 - c)


def send(value, pairs):
    return lax.ppermute(value, AXES, pairs)


def join(*parts):
    return jnp.concatenate(parts, axis=0)


def contract_last(left, right):
    return lax.dot_general(
        left, right, (((1,), (1,)), ((), ())), preferred_element_type=jnp.float32
    )


def contract_first(left, right):
    return lax.dot_general(
        left, right, (((0,), (0,)), ((), ())), preferred_element_type=jnp.float32
    )


def matmul(left, right):
    return jnp.dot(left, right, preferred_element_type=jnp.float32)


def half(v):
    return v.astype(jnp.bfloat16)


def full(v):
    return v.astype(jnp.float32)


SMALL = pl.CostEstimate(flops=1 << 36, bytes_accessed=1 << 30, transcendentals=0)
GAP = 384
FWD, TERM, SUMS = 14, 10, 24
ON_CHIP = pl.BlockSpec(memory_space=pltpu.VMEM)


def forward(pair, other, gate, up, down):
    tile = 1024
    m, (units, width) = pair.shape[0] // 2, gate.shape

    def kernel(pair_ref, other_ref, gate_ref, up_ref, down_ref, hidden_ref, grads_ref, acc):
        acc[...] = jnp.zeros_like(acc)

        @pl.loop(0, width // tile)
        def _(step):
            at = pl.ds(pl.multiple_of(step * tile, tile), tile)
            rows_acts = join(pair_ref[:m, at], other_ref[:m, at])
            rows_grads = join(pair_ref[m:, at], other_ref[m:, at])
            acc[0] += contract_last(gate_ref[:, at], rows_acts)
            acc[1] += contract_last(up_ref[:, at], rows_acts)
            acc[2] += contract_last(down_ref[:, at], rows_grads)

        gate_pre, up_pre, hidden_grad = acc[0], acc[1], acc[2]
        sig_gate = jax.nn.sigmoid(gate_pre)
        silu_gate = gate_pre * sig_gate
        hidden_ref[...] = half(silu_gate * up_pre)
        grads_ref[:units, :] = half(
            hidden_grad * up_pre * sig_gate * (1.0 + gate_pre * (1.0 - sig_gate))
        )
        grads_ref[GAP : GAP + units, :] = half(hidden_grad * silu_gate)
        blank = jnp.zeros((GAP - units, 2 * m), jnp.bfloat16)
        grads_ref[units:GAP, :] = blank
        grads_ref[GAP + units :, :] = blank

    return pl.pallas_call(
        kernel,
        in_specs=[ON_CHIP] * 5,
        out_specs=[ON_CHIP] * 2,
        out_shape=[
            jax.ShapeDtypeStruct((units, 2 * m), jnp.bfloat16),
            jax.ShapeDtypeStruct((2 * GAP, 2 * m), jnp.bfloat16),
        ],
        scratch_shapes=[pltpu.VMEM((3, units, 2 * m), jnp.float32)],
        compiler_params=pltpu.CompilerParams(vmem_limit_bytes=FWD << 20),
        cost_estimate=SMALL,
    )(pair, other, gate, up, down)


def input_terms(grads, gate, up):
    tile = 512
    n, (units, width) = grads.shape[1], gate.shape
    m = n // 2

    def kernel(grads_ref, gate_ref, up_ref, own_ref, other_ref, left, right):
        left[...] = grads_ref[...].T
        right[...] = jnp.zeros_like(right)

        @pl.loop(0, width // tile)
        def _(step):
            at = pl.ds(pl.multiple_of(step * tile, tile), tile)
            right[:units, :] = gate_ref[:, at]
            right[GAP : GAP + units, :] = up_ref[:, at]
            term = half(matmul(left[...], right[...]))
            own_ref[:, at] = term[:m]
            other_ref[:, at] = term[m:]

    return pl.pallas_call(
        kernel,
        in_specs=[ON_CHIP] * 3,
        out_specs=[ON_CHIP] * 2,
        out_shape=[jax.ShapeDtypeStruct((m, width), jnp.bfloat16)] * 2,
        scratch_shapes=[
            pltpu.VMEM((n, 2 * GAP), jnp.bfloat16),
            pltpu.VMEM((2 * GAP, tile), jnp.bfloat16),
        ],
        compiler_params=pltpu.CompilerParams(vmem_limit_bytes=TERM << 20),
        cost_estimate=SMALL,
    )(grads, gate, up)


def weight_grads(pairs, hiddens, grads, first, count, earlier):
    tile = 512
    n = len(pairs)
    units, width = hiddens[0].shape[0], pairs[0].shape[1]
    total = sum(p.shape[0] for p in pairs) // 2
    kept = len(earlier)

    def kernel(*refs):
        pair_refs, hidden_refs, grads_refs = refs[:n], refs[n : n + n // 2], refs[n + n // 2 : 2 * n]
        gate_out, up_out, down_out = refs[2 * n + kept : 2 * n + kept + 3]
        acts, rows_grads, hidden, grad, sems = refs[2 * n + kept + 3 :]
        step = pl.program_id(0)

        def copies(at, slot):
            columns = pl.ds(pl.multiple_of((first + at) * tile, tile), tile)
            made, start = [], 0
            for k in range(n):
                m = pairs[k].shape[0] // 2
                for part, dst in ((0, acts), (1, rows_grads)):
                    made.append(
                        pltpu.make_async_copy(
                            pair_refs[k].at[pl.ds(part * m, m), columns],
                            dst.at[slot, pl.ds(start, m), :],
                            sems.at[slot, 2 * k + part],
                        )
                    )
                start += m
            return made

        @pl.when(step == 0)
        def _():
            for c in copies(0, 0):
                c.start()
            start = 0
            for k in range(n // 2):
                m = hidden_refs[k].shape[1]
                hidden[:, start : start + m] = hidden_refs[k][...]
                grad[:, start : start + m] = grads_refs[k][...]
                start += m

        slot = lax.rem(step, 2)

        @pl.when(step + 1 < count)
        def _():
            for c in copies(step + 1, 1 - slot):
                c.start()

        for c in copies(step, slot):
            c.wait()
        right = acts[slot]
        gate_out[...] = half(matmul(grad[:units, :], right))
        up_out[...] = half(matmul(grad[GAP : GAP + units, :], right))
        down_out[...] = half(matmul(hidden[...], rows_grads[slot]))

    whole = [
        pl.BlockSpec(v.shape, lambda j: (0, 0), pipeline_mode=pl.Buffered(1)) for v in hiddens + grads
    ]
    hbm = pl.BlockSpec(memory_space=pl.ANY)
    return pl.pallas_call(
        kernel,
        grid=(count,),
        in_specs=[hbm] * n + whole + [hbm] * kept,
        out_specs=[pl.BlockSpec((units, tile), lambda j: (0, first + j))] * 3,
        out_shape=[jax.ShapeDtypeStruct((units, width), jnp.bfloat16)] * 3,
        input_output_aliases={2 * n + i: i for i in range(kept)},
        scratch_shapes=[
            pltpu.VMEM((2, total, tile), jnp.bfloat16),
            pltpu.VMEM((2, total, tile), jnp.bfloat16),
            pltpu.VMEM((units, total), jnp.bfloat16),
            pltpu.VMEM((2 * GAP, total), jnp.bfloat16),
            pltpu.SemaphoreType.DMA((2, 2 * n)),
        ],
        compiler_params=pltpu.CompilerParams(vmem_limit_bytes=SUMS << 20),
        cost_estimate=SMALL,
    )(*pairs, *hiddens, *grads, *earlier)


def together(*values):
    return lax.optimization_barrier(values)


def per_device(
    activations, upstream_grad, routes, router_probs, gate_weight, up_weight, down_weight
):
    local_acts = activations[0, 0]
    local_grads = upstream_grad[0, 0]
    expert_hits = routes[0, 0] == 0
    router_weight = jnp.sum(jnp.where(expert_hits, router_probs[0, 0], jnp.float32(0.0)), axis=1)
    is_routed = jnp.any(expert_hits, axis=1)
    before = jnp.arange(256)[None, :] <= jnp.arange(256)[:, None]
    count = jnp.sum(jnp.where(before & is_routed[None, :], 1, 0), axis=1)
    slot = jnp.where(is_routed, count, 0)
    wanted = jnp.arange(1, CAP + 1, dtype=jnp.int32)
    picker = half(slot[None, :] == wanted[:, None])
    scaled = half(router_weight[:, None] * full(local_grads))
    a = half(matmul(picker, local_acts))
    g = half(matmul(picker, scaled))
    gate_local, up_local, down_local = gate_weight[0], up_weight[0], down_weight[0]

    weights = (gate_local, up_local, down_local)

    a, g = together(a, g)
    a_is, a_os, g_sb, g_su = send(a, INNER), send(a, OUTER), send(g, UP), send(g, DOWN)
    to_i, to_o, to_u, to_b, slot_out, a, g = together(
        join(a_os[:32], g, g_sb, g_su),
        join(a_is[32:], g, g_sb, g_su),
        join(g_sb[:32], a, a_is, a_os),
        join(g_su[32:], a, a_is, a_os),
        slot,
        a,
        g,
    )
    from_i, from_o, from_b, from_u = send(to_i, INNER), send(to_o, OUTER), send(to_u, UP), send(to_b, DOWN)
    next_slot = lax.ppermute(slot_out, "section", [(1, 0), (2, 1), (3, 2)])
    own_pair = join(
        a, a_is, from_b[32:160], from_u[32:160],
        g, from_i[32:96], g_sb, from_i[96:160], g_su, from_i[160:224],
    )
    a_ts, g_st = join(from_i[:32], from_o[:32]), join(from_b[:32], from_u[:32])
    own_pair, g_st, a_sb, a_iu, next_slot, from_i, from_o, from_b, from_u = together(
        own_pair, g_st, from_b[32:96], from_u[96:160], next_slot, from_i, from_o, from_b, from_u
    )
    g_it, g_ot, a_st, a_it = send(g_st, INNER), send(g_st, OUTER), send(a_sb, UP), send(a_iu, DOWN)
    own_other = send(own_pair, SIBLING)
    far_pair = join(a_st, a_it, g_st, g_it)
    to_i, to_o, a_ts, far_pair, own_pair, own_other, g_ot, a_it, from_o, from_b, from_u = together(
        from_o[96:192], join(from_i[192:224], g_it), a_ts, far_pair, own_pair, own_other, g_ot, a_it,
        from_o, from_b, from_u,
    )
    far_other = send(far_pair, SIBLING)
    g_i, g_o, a_tb, a_tu = send(to_i, INNER), send(to_o, OUTER), send(a_ts, UP), send(a_ts, DOWN)
    hidden_far, grads_far = forward(far_pair, far_other, *weights)
    term_far, term_far2 = input_terms(grads_far, gate_local, up_local)
    far_from = send(term_far2, SIBLING)
    hidden_own, grads_own = forward(own_pair, own_other, *weights)
    g_i, g_o, a_tb, a_tu, far_from, grads_own, to_i, to_o, to_u, to_b = together(
        g_i, g_o, a_tb, a_tu, far_from, grads_own, from_o[32:96], a_it, from_b[160:192], from_u[192:224]
    )
    g_ts, a_tt, a_ot1, a_ot2 = send(to_i, INNER), send(to_o, OUTER), send(to_u, UP), send(to_b, DOWN)
    term_own, term_own2 = input_terms(grads_own, gate_local, up_local)
    term_from = send(term_own2, SIBLING)
    far = half(full(term_far) + full(far_from))
    own = half(full(term_own) + full(term_from))
    x1_pair = join(a_os, from_b[160:224], from_u[160:224], from_o[32:224])
    x2_pair = join(a_tb, a_tu, g_i, g_o[:32])
    to_b, to_u, to_i, own0, far0, a_ot1, a_ot2, a_ts, g_ot, g_ts, a_tt, x1_pair, x2_pair = together(
        own[128:256], own[256:384], far[64:128], own[:128], far[:64],
        a_ot1, a_ot2, a_ts, g_ot, g_ts, a_tt, x1_pair, x2_pair,
    )
    z_u, z_b, far_i = send(to_b, DOWN), send(to_u, UP), send(to_i, INNER)
    x3_pair = join(a_ot1, a_ot2, a_ts, a_tt, g_ot, g_ts, g_o[32:])
    x1_other, x2_other, x3_other = send(x1_pair, SIBLING), send(x2_pair, SIBLING), send(x3_pair, SIBLING)
    hidden_x1, grads_x1 = forward(x1_pair, x1_other, *weights)
    hidden_x2, grads_x2 = forward(x2_pair, x2_other, *weights)
    hidden_x3, grads_x3 = forward(x3_pair, x3_other, *weights)
    z_u, z_b, far_i, hidden_x1, hidden_x2, hidden_x3 = together(
        z_u, z_b, far_i, hidden_x1, hidden_x2, hidden_x3
    )
    near = full(own0) + full(z_u) + full(z_b)
    to_i, to_t, near_s = together(half(near[64:]), half(full(far0) + full(far_i)), near[:64])
    near_i, far_t = send(to_i, INNER), send(to_t, ACROSS)
    pairs = [
        own_pair, own_other, far_pair, far_other,
        x1_pair, x1_other, x2_pair, x2_other, x3_pair, x3_other,
    ]
    hiddens = [hidden_own, hidden_far, hidden_x1, hidden_x2, hidden_x3]
    grads = [grads_own, grads_far, grads_x1, grads_x2, grads_x3]
    early = weight_grads(pairs, hiddens, grads, 0, 4, ())
    input_rows, early = together(half(near_s + full(near_i) + full(far_t)), tuple(early))
    shifted = lax.ppermute(input_rows, "section", [(1, 0), (2, 1), (3, 2)])
    placer = half(next_slot[:, None] == wanted[None, :])
    grad_gate, grad_up, grad_down = weight_grads(pairs, hiddens, grads, 4, 4, early)
    prev_grad = half(matmul(placer, shifted))[None, None]
    return (grad_gate[None], grad_up[None], grad_down[None], prev_grad)


def solution(mesh):
    placed = (
        P("cuts", "section", "dp", None),
        P("cuts", "section", "dp", None),
        P("cuts", "section", "dp", None),
        P("cuts", "section", "dp", None),
        P("section", "dp", None),
        P("section", "dp", None),
        P("section", "dp", None),
    )
    return jax.shard_map(
        per_device,
        mesh=mesh,
        in_specs=placed,
        out_specs=(
            P("section", "dp", None),
            P("section", "dp", None),
            P("section", "dp", None),
            P("cuts", "section", "dp", None),
        ),
        check_vma=False,
    )
```

profile of v0, /device:TPU:12, one launch (start us, length us, event | category | flops | bytes accessed | tf_op | source)
XLA Modules:
  0.0 203.7 jit_solution(14556146186143344191)
XLA Ops:
  0.7 0.9 select_reduce_fusion.1
  1.7 0.6 copy-done
  2.8 2.2 %convolution_convert_fusion.1 = bf16[64,4096]{1,0:T(8,128)(2,1)S(1)} fusion(bf16[1,1,256,4096]{3,2,1,0:T(8,128)(2,1)} %param.8, f32[256]{0:T(256)S(1)} %get-tuple-element.174, s32[256]{0:T(256)S(1)} %broadcast_select_fusion, s32[64]{0:T(128)S(1)} %iota_add_fusion), kind=kOutput, calls=%fused_computation.3 | convolution fusion | flops 137641984 | bytes 2623744 | tf_op jit(solution)/shard_map/dot_general | solution.py:58
  5.0 1.3 collective-permute-start.3
  6.3 4.0 %collective-permute-start.2 = (bf16[64,4096]{1,0:T(8,128)(2,1)S(1)}, bf16[64,4096]{1,0:T(8,128)(2,1)S(1)}, u32[]{:S(2)}, u32[]{:S(2)}) collective-permute-start(bf16[64,4096]{1,0:T(8,128)(2,1)S(1)} %convolution_convert_fusion.1), channel_id=1, source_target_pairs={{0,12},{1,13},{4,0},{5,1},{8,4},{9,5},{12,8},{13,9},{2,14},{3,15},... | collective-permute-start | bytes 1572872 | tf_op jit(solution)/shard_map/ppermute | solution.py:38
  10.3 8.4 %collective-permute-done.3 = bf16[64,4096]{1,0:T(8,128)(2,1)S(1)} collective-permute-done((bf16[64,4096]{1,0:T(8,128)(2,1)S(1)}, bf16[64,4096]{1,0:T(8,128)(2,1)S(1)}, u32[]{:S(2)}, u32[]{:S(2)}) %collective-permute-start.3) | collective-permute-done | bytes 524320 | tf_op jit(solution)/shard_map/ppermute | solution.py:38
  18.8 0.9 collective-permute-done
  19.7 1.5 collective-permute-done.2
  21.3 3.4 %collective-permute-done.1 = bf16[64,4096]{1,0:T(8,128)(2,1)S(1)} collective-permute-done((bf16[64,4096]{1,0:T(8,128)(2,1)S(1)}, bf16[64,4096]{1,0:T(8,128)(2,1)S(1)}, u32[]{:S(2)}, u32[]{:S(2)}) %collective-permute-start.1) | collective-permute-done | bytes 524320 | tf_op jit(solution)/shard_map/ppermute | solution.py:38
  24.7 1.0 pad_maximum_fusion.1
  25.8 2.4 %collective-permute-start.7 = (s32[256]{0:T(256)S(1)}, s32[256]{0:T(256)S(1)}, u32[]{:S(2)}, u32[]{:S(2)}) collective-permute-start(s32[256]{0:T(256)S(1)} %broadcast_select_fusion), channel_id=1, source_target_pairs={{16,0},{32,16},{48,32},{17,1},{33,17},{49,33},{18,2},{34,18},{50,3... | collective-permute-start | bytes 3080 | tf_op jit(solution)/shard_map/ppermute | solution.py:262
  28.1 3.3 %collective-permute-start.5 = (bf16[224,4096]{1,0:T(8,128)(2,1)S(1)}, bf16[224,4096]{1,0:T(8,128)(2,1)S(1)}, u32[]{:S(2)}, u32[]{:S(2)}) collective-permute-start(bf16[224,4096]{1,0:T(8,128)(2,1)S(1)} %get-tuple-element.93), channel_id=1, source_target_pairs={{0,12},{1,13},{4,0},{5,1},{8,4},{9,5},{12,8},{13,9},{2,14},{3,15},... | collective-permute-start | bytes 5505032 | tf_op jit(solution)/shard_map/ppermute | solution.py:38
  31.4 1.7 collective-permute-start.6
  33.1 1.5 collective-permute-start.8
  34.7 32.6 %collective-permute-done.4 = bf16[224,4096]{1,0:T(8,128)(2,1)S(1)} collective-permute-done((bf16[224,4096]{1,0:T(8,128)(2,1)S(1)}, bf16[224,4096]{1,0:T(8,128)(2,1)S(1)}, u32[]{:S(2)}, u32[]{:S(2)}) %collective-permute-start.4) | collective-permute-done | bytes 1835040 | tf_op jit(solution)/shard_map/ppermute | solution.py:38
  67.3 1.3 collective-permute-done.5
  68.8 2.0 %collective-permute-done.6 = bf16[224,4096]{1,0:T(8,128)(2,1)S(1)} collective-permute-done((bf16[224,4096]{1,0:T(8,128)(2,1)S(1)}, bf16[224,4096]{1,0:T(8,128)(2,1)S(1)}, u32[]{:S(2)}, u32[]{:S(2)}) %collective-permute-start.6) | collective-permute-done | bytes 1835040 | tf_op jit(solution)/shard_map/ppermute | solution.py:38
  71.1 0.7 slice-done.1
  71.8 0.6 copy-done.20
  72.7 1.5 collective-permute-start.9
  74.2 1.5 collective-permute-start.13
  75.6 3.2 %collective-permute-start.11 = (bf16[64,4096]{1,0:T(8,128)(2,1)S(1)}, bf16[64,4096]{1,0:T(8,128)(2,1)S(1)}, u32[]{:S(2)}, u32[]{:S(2)}) collective-permute-start(bf16[64,4096]{1,0:T(8,128)(2,1)S(1)} %slice.141), channel_id=1, source_target_pairs={{0,12},{1,13},{4,0},{5,1},{8,4},{9,5},{12,8},{13,9},{2,14},{3,15},... | collective-permute-start | bytes 1572872 | tf_op jit(solution)/shard_map/ppermute | solution.py:38
  78.9 0.8 pad_maximum_fusion.17
  79.8 1.0 slice.110
  80.8 6.3 %collective-permute-done.9 = bf16[64,4096]{1,0:T(8,128)(2,1)S(1)} collective-permute-done((bf16[64,4096]{1,0:T(8,128)(2,1)S(1)}, bf16[64,4096]{1,0:T(8,128)(2,1)S(1)}, u32[]{:S(2)}, u32[]{:S(2)}) %collective-permute-start.9) | collective-permute-done | bytes 524320 | tf_op jit(solution)/shard_map/ppermute | solution.py:38
  87.0 1.0 pad_maximum_fusion.15
  88.0 2.6 %collective-permute-done.10 = bf16[64,4096]{1,0:T(8,128)(2,1)S(1)} collective-permute-done((bf16[64,4096]{1,0:T(8,128)(2,1)S(1)}, bf16[64,4096]{1,0:T(8,128)(2,1)S(1)}, u32[]{:S(2)}, u32[]{:S(2)}) %collective-permute-start.10) | collective-permute-done | bytes 524320 | tf_op jit(solution)/shard_map/ppermute | solution.py:38
  90.9 3.0 %collective-permute-start.18 = (bf16[64,4096]{1,0:T(8,128)(2,1)}, bf16[64,4096]{1,0:T(8,128)(2,1)}, u32[]{:S(2)}, u32[]{:S(2)}) collective-permute-start(bf16[64,4096]{1,0:T(8,128)(2,1)} %pad_maximum_fusion.17), channel_id=1, source_target_pairs={{0,12},{1,13},{4,0},{5,1},{8,4},{9,5},{12,8},{13,9},{2,14},{3,15},... | collective-permute-start | bytes 1572872 | tf_op jit(solution)/shard_map/ppermute | solution.py:38
  94.0 1.2 collective-permute-start.15
  95.7 3.2 %shard_map.102 = (bf16[336,256]{1,0:T(8,128)(2,1)S(1)}, bf16[768,256]{1,0:T(8,128)(2,1)S(1)}) custom-call(bf16[256,4096]{1,0:T(8,128)(2,1)S(1)} %pad_maximum_fusion.13.pair_ref.refs_2_, bf16[256,4096]{1,0:T(8,128)(2,1)S(1)} %collective-permute-done.14.other_ref.refs_3_, bf16[336,4096]{1,0:T(8,128)(2,1)S(1)} %bitcast.18, bf16[336,4096]{1,0:T(8,128)(2,1)S(1)} %bitcast.25, ...), custom_call_target="tpu_custom_call" | custom-call | flops 68719476736 | bytes 1073741824 | tf_op jit(solution)/shard_map/pallas_call | solution.py:103
  99.0 3.2 %shard_map.103 = (bf16[128,4096]{1,0:T(8,128)(2,1)S(1)}, bf16[128,4096]{1,0:T(8,128)(2,1)S(1)}) custom-call(bf16[768,256]{1,0:T(8,128)(2,1)S(1)} %get-tuple-element.112.grads_ref.refs_16_, bf16[336,4096]{1,0:T(8,128)(2,1)S(1)} %bitcast.19, bf16[336,4096]{1,0:T(8,128)(2,1)S(1)} %bitcast.26), custom_call_target="tpu_custom_call" | custom-call | flops 68719476736 | bytes 1073741824 | tf_op jit(solution)/shard_map/pallas_call | solution.py:135
  102.5 8.1 %shard_map.104 = (bf16[336,768]{1,0:T(8,128)(2,1)S(1)}, bf16[768,768]{1,0:T(8,128)(2,1)S(1)}) custom-call(bf16[768,4096]{1,0:T(8,128)(2,1)S(1)} %slice_dynamic-update-slice_fusion.2.pair_ref.refs_0_, bf16[768,4096]{1,0:T(8,128)(2,1)S(1)} %collective-permute-done.12.other_ref.refs_1_, bf16[336,4096]{1,0:T(8,128)(2,1)S(1)} %bitcast.20, ...), custom_call_target="tpu_custom_call" | custom-call | flops 68719476736 | bytes 1073741824 | tf_op jit(solution)/shard_map/pallas_call | solution.py:103
  110.8 3.1 %collective-permute-done.15 = bf16[96,4096]{1,0:T(8,128)(2,1)} collective-permute-done((bf16[96,4096]{1,0:T(8,128)(2,1)}, bf16[96,4096]{1,0:T(8,128)(2,1)}, u32[]{:S(2)}, u32[]{:S(2)}) %collective-permute-start.15) | collective-permute-done | bytes 786464 | tf_op jit(solution)/shard_map/ppermute | solution.py:38
  113.9 0.9 collective-permute-done.16
  114.8 1.0 copy-done.27
  115.8 6.6 %shard_map.105 = (bf16[384,4096]{1,0:T(8,128)(2,1)S(1)}, bf16[384,4096]{1,0:T(8,128)(2,1)S(1)}) custom-call(bf16[768,768]{1,0:T(8,128)(2,1)S(1)} %get-tuple-element.119.grads_ref.refs_15_, bf16[336,4096]{1,0:T(8,128)(2,1)S(1)} %bitcast.21, bf16[336,4096]{1,0:T(8,128)(2,1)S(1)} %bitcast.28), custom_call_target="tpu_custom_call" | custom-call | flops 68719476736 | bytes 1073741824 | tf_op jit(solution)/shard_map/pallas_call | solution.py:135
  122.5 1.3 slice-done
  124.5 1.1 slice.125
  125.7 3.2 %collective-permute-start.22 = (bf16[32,4096]{1,0:T(8,128)(2,1)S(1)}, bf16[32,4096]{1,0:T(8,128)(2,1)S(1)}, u32[]{:S(2)}, u32[]{:S(2)}) collective-permute-start(bf16[32,4096]{1,0:T(8,128)(2,1)S(1)} %slice.116), channel_id=1, source_target_pairs={{0,12},{1,13},{4,0},{5,1},{8,4},{9,5},{12,8},{13,9},{2,14},{3,15},... | collective-permute-start | bytes 786440 | tf_op jit(solution)/shard_map/ppermute | solution.py:38
  128.9 2.0 collective-permute-start.23
  131.5 1.6 pad_maximum_fusion.14.pair_ref.refs_6_
  133.4 1.0 fusion.17
  134.4 1.2 add_convert_fusion
  135.6 1.8 fusion.16
  137.4 4.1 %collective-permute-done.23 = bf16[64,4096]{1,0:T(8,128)(2,1)S(1)} collective-permute-done((bf16[64,4096]{1,0:T(8,128)(2,1)S(1)}, bf16[64,4096]{1,0:T(8,128)(2,1)S(1)}, u32[]{:S(2)}, u32[]{:S(2)}) %collective-permute-start.23) | collective-permute-done | bytes 524320 | tf_op jit(solution)/shard_map/ppermute | solution.py:38
  141.5 1.5 collective-permute-done.24
  142.9 1.5 collective-permute-start.30
  144.4 1.6 collective-permute-start.28
  146.5 1.1 constant_dynamic-update-slice_fusion.8
  147.7 1.1 slice_dynamic-update-slice_fusion.5.pair_ref.refs_8_
  148.8 0.6 collective-permute-start.27
  149.4 1.2 collective-permute-done.26.other_ref.refs_7_
  150.8 3.2 %shard_map.107 = (bf16[336,256]{1,0:T(8,128)(2,1)S(1)}, bf16[768,256]{1,0:T(8,128)(2,1)S(1)}) custom-call(bf16[256,4096]{1,0:T(8,128)(2,1)S(1)} %pad_maximum_fusion.14.pair_ref.refs_6_, bf16[256,4096]{1,0:T(8,128)(2,1)S(1)} %collective-permute-done.26.other_ref.refs_7_, bf16[336,4096]{1,0:T(8,128)(2,1)S(1)} %bitcast.22, bf16[336,4096]{1,0:T(8,128)(2,1)S(1)} %bitcast.29, ...), custom_call_target="tpu_custom_call" | custom-call | flops 68719476736 | bytes 1073741824 | tf_op jit(solution)/shard_map/pallas_call | solution.py:103
  154.0 1.1 collective-permute-done.27.other_ref.refs_9_
  155.1 5.4 %shard_map.108 = (bf16[336,384]{1,0:T(8,128)(2,1)S(1)}, bf16[768,384]{1,0:T(8,128)(2,1)S(1)}) custom-call(bf16[384,4096]{1,0:T(8,128)(2,1)S(1)} %slice_dynamic-update-slice_fusion.5.pair_ref.refs_8_, bf16[384,4096]{1,0:T(8,128)(2,1)S(1)} %collective-permute-done.27.other_ref.refs_9_, bf16[336,4096]{1,0:T(8,128)(2,1)S(1)} %bitcast.23, ...), custom_call_target="tpu_custom_call" | custom-call | flops 68719476736 | bytes 1073741824 | tf_op jit(solution)/shard_map/pallas_call | solution.py:103
  160.6 5.4 %shard_map.106 = (bf16[336,384]{1,0:T(8,128)(2,1)S(1)}, bf16[768,384]{1,0:T(8,128)(2,1)S(1)}) custom-call(bf16[384,4096]{1,0:T(8,128)(2,1)S(1)} %pad_maximum_fusion.pair_ref.refs_4_, bf16[384,4096]{1,0:T(8,128)(2,1)S(1)} %collective-permute-done.25.other_ref.refs_5_, bf16[336,4096]{1,0:T(8,128)(2,1)S(1)} %bitcast.24, bf16[336,4096]{1,0:T(8,128)(2,1)S(1)} %bitcast.31, ...), custom_call_target="tpu_custom_call" | custom-call | flops 68719476736 | bytes 1073741824 | tf_op jit(solution)/shard_map/pallas_call | solution.py:103
  166.0 1.1 collective-permute-done.28
  167.1 2.3 %collective-permute-done.29 = bf16[128,4096]{1,0:T(8,128)(2,1)} collective-permute-done((bf16[128,4096]{1,0:T(8,128)(2,1)}, bf16[128,4096]{1,0:T(8,128)(2,1)}, u32[]{:S(2)}, u32[]{:S(2)}) %collective-permute-start.29) | collective-permute-done | bytes 1048608 | tf_op jit(solution)/shard_map/ppermute | solution.py:38
  169.4 2.1 %convert_add_fusion = f32[128,4096]{1,0:T(8,128)S(1)} fusion(bf16[128,4096]{1,0:T(8,128)(2,1)} %collective-permute-done.29, bf16[128,4096]{1,0:T(8,128)(2,1)} %collective-permute-done.28, bf16[128,4096]{1,0:T(8,128)(2,1)S(1)} %copy-done.18), kind=kLoop, calls=%fused_computation.24 | loop fusion | flops 2621440 | bytes 5242880 | tf_op jit(solution)/shard_map/add | solution.py:307
  171.7 1.3 add_convert_fusion.3
  173.9 12.6 %shard_map.109 = (bf16[336,4096]{1,0:T(8,128)(2,1)}, bf16[336,4096]{1,0:T(8,128)(2,1)}, bf16[336,4096]{1,0:T(8,128)(2,1)}) custom-call(bf16[768,4096]{1,0:T(8,128)(2,1)} %copy-done.4, bf16[768,4096]{1,0:T(8,128)(2,1)} %copy-done.5, bf16[256,4096]{1,0:T(8,128)(2,1)S(1)} %copy-done.3, bf16[256,4096]{1,0:T(8,128)(2,1)S(1)} %copy-done.11, ...), custom_call_target="tpu_custom_call" | custom-call | flops 68719476736 | bytes 1073741824 | tf_op jit(solution)/shard_map/pallas_call | solution.py:207
  186.8 1.9 collective-permute-start.33
  188.8 12.8 %shard_map.110 = (bf16[336,4096]{1,0:T(8,128)(2,1)}, bf16[336,4096]{1,0:T(8,128)(2,1)}, bf16[336,4096]{1,0:T(8,128)(2,1)}) custom-call(bf16[768,4096]{1,0:T(8,128)(2,1)} %copy-done.4, bf16[768,4096]{1,0:T(8,128)(2,1)} %copy-done.5, bf16[256,4096]{1,0:T(8,128)(2,1)S(1)} %copy-done.3, ...), custom_call_target="tpu_custom_call", output_to_operand_aliasing={{0}: (20, {}), {1}: (21, {}), {2}: (22, {})} | custom-call | flops 68719476736 | bytes 1073741824 | tf_op jit(solution)/shard_map/pallas_call | solution.py:207
  201.6 2.1 %fusion = bf16[1,1,256,4096]{3,2,1,0:T(8,128)(2,1)} fusion(bf16[64,4096]{1,0:T(8,128)(2,1)S(1)} %collective-permute-done.33, s32[64]{0:T(128)S(1)} %copy-done.34, s32[256]{0:T(256)S(1)} %copy-done.36), kind=kOutput, calls=%fused_computation.2 | convolution fusion | flops 135282688 | bytes 2622720 | tf_op jit(solution)/shard_map/dot_general | solution.py:58
  (151 shorter events, 6.5 us)
Async XLA Ops:
  0.7 19.0 %copy-start.33 = (s32[64]{0:T(128)}, s32[64]{0:T(128)S(1)}, u32[]{:S(2)}) copy-start(s32[64]{0:T(128)S(1)} %iota_add_fusion) | copy-start | bytes 772
  5.0 13.7 %collective-permute-start.3 = (bf16[64,4096]{1,0:T(8,128)(2,1)S(1)}, bf16[64,4096]{1,0:T(8,128)(2,1)S(1)}, u32[]{:S(2)}, u32[]{:S(2)}) collective-permute-start(bf16[64,4096]{1,0:T(8,128)(2,1)S(1)} %convolution_convert_fusion.2), channel_id=1, source_target_pairs={{0,2},{1,3},{4,6},{5,7},{8,10},{9,11},{12,14},{13,15},{2,0},{3,1},... | collective-permute-start | bytes 1572872 | tf_op jit(solution)/shard_map/ppermute | solution.py:38
  6.3 13.4 %collective-permute-start = (bf16[64,4096]{1,0:T(8,128)(2,1)S(1)}, bf16[64,4096]{1,0:T(8,128)(2,1)S(1)}, u32[]{:S(2)}, u32[]{:S(2)}) collective-permute-start(bf16[64,4096]{1,0:T(8,128)(2,1)S(1)} %convolution_convert_fusion.2), channel_id=1, source_target_pairs={{0,66},{1,67},{4,70},{5,71},{8,74},{9,75},{12,78},{13,79},{2,64},{... | collective-permute-start | bytes 1572872 | tf_op jit(solution)/shard_map/ppermute | solution.py:38
  6.3 14.9 %collective-permute-start.2 = (bf16[64,4096]{1,0:T(8,128)(2,1)S(1)}, bf16[64,4096]{1,0:T(8,128)(2,1)S(1)}, u32[]{:S(2)}, u32[]{:S(2)}) collective-permute-start(bf16[64,4096]{1,0:T(8,128)(2,1)S(1)} %convolution_convert_fusion.1), channel_id=1, source_target_pairs={{0,12},{1,13},{4,0},{5,1},{8,4},{9,5},{12,8},{13,9},{2,14},{3,15},... | collective-permute-start | bytes 1572872 | tf_op jit(solution)/shard_map/ppermute | solution.py:38
  10.3 14.3 %collective-permute-start.1 = (bf16[64,4096]{1,0:T(8,128)(2,1)S(1)}, bf16[64,4096]{1,0:T(8,128)(2,1)S(1)}, u32[]{:S(2)}, u32[]{:S(2)}) collective-permute-start(bf16[64,4096]{1,0:T(8,128)(2,1)S(1)} %convolution_convert_fusion.1), channel_id=1, source_target_pairs={{0,4},{1,5},{4,8},{5,9},{8,12},{9,13},{12,0},{13,1},{2,6},{3,7},{6... | collective-permute-start | bytes 1572872 | tf_op jit(solution)/shard_map/ppermute | solution.py:38
  19.7 6.0 %copy-start.24 = (bf16[64,4096]{1,0:T(8,128)(2,1)}, bf16[64,4096]{1,0:T(8,128)(2,1)S(1)}, u32[]{:S(2)}) copy-start(bf16[64,4096]{1,0:T(8,128)(2,1)S(1)} %collective-permute-done) | copy-start | bytes 1572868
  25.7 41.6 %collective-permute-start.4 = (bf16[224,4096]{1,0:T(8,128)(2,1)S(1)}, bf16[224,4096]{1,0:T(8,128)(2,1)S(1)}, u32[]{:S(2)}, u32[]{:S(2)}) collective-permute-start(bf16[224,4096]{1,0:T(8,128)(2,1)S(1)} %get-tuple-element.92), channel_id=1, source_target_pairs={{0,4},{1,5},{4,8},{5,9},{8,12},{9,13},{12,0},{13,1},{2,6},{3,7},{6... | collective-permute-start | bytes 5505032 | tf_op jit(solution)/shard_map/ppermute | solution.py:38
  25.8 46.8 %collective-permute-start.7 = (s32[256]{0:T(256)S(1)}, s32[256]{0:T(256)S(1)}, u32[]{:S(2)}, u32[]{:S(2)}) collective-permute-start(s32[256]{0:T(256)S(1)} %broadcast_select_fusion), channel_id=1, source_target_pairs={{16,0},{32,16},{48,32},{17,1},{33,17},{49,33},{18,2},{34,18},{50,3... | collective-permute-start | bytes 3080 | tf_op jit(solution)/shard_map/ppermute | solution.py:262
  28.1 40.5 %collective-permute-start.5 = (bf16[224,4096]{1,0:T(8,128)(2,1)S(1)}, bf16[224,4096]{1,0:T(8,128)(2,1)S(1)}, u32[]{:S(2)}, u32[]{:S(2)}) collective-permute-start(bf16[224,4096]{1,0:T(8,128)(2,1)S(1)} %get-tuple-element.93), channel_id=1, source_target_pairs={{0,12},{1,13},{4,0},{5,1},{8,4},{9,5},{12,8},{13,9},{2,14},{3,15},... | collective-permute-start | bytes 5505032 | tf_op jit(solution)/shard_map/ppermute | solution.py:38
  31.4 39.4 %collective-permute-start.6 = (bf16[224,4096]{1,0:T(8,128)(2,1)S(1)}, bf16[224,4096]{1,0:T(8,128)(2,1)S(1)}, u32[]{:S(2)}, u32[]{:S(2)}) collective-permute-start(bf16[224,4096]{1,0:T(8,128)(2,1)S(1)} %get-tuple-element.95), channel_id=1, source_target_pairs={{0,2},{1,3},{4,6},{5,7},{8,10},{9,11},{12,14},{13,15},{2,0},{3,1},... | collective-permute-start | bytes 5505032 | tf_op jit(solution)/shard_map/ppermute | solution.py:38
  33.1 39.5 %collective-permute-start.8 = (bf16[224,4096]{1,0:T(8,128)(2,1)S(1)}, bf16[224,4096]{1,0:T(8,128)(2,1)S(1)}, u32[]{:S(2)}, u32[]{:S(2)}) collective-permute-start(bf16[224,4096]{1,0:T(8,128)(2,1)S(1)} %get-tuple-element.97), channel_id=1, source_target_pairs={{0,66},{1,67},{4,70},{5,71},{8,74},{9,75},{12,78},{13,79},{2,64},{... | collective-permute-start | bytes 5505032 | tf_op jit(solution)/shard_map/ppermute | solution.py:38
  68.6 3.8 %copy-start.22 = (bf16[224,4096]{1,0:T(8,128)(2,1)}, bf16[224,4096]{1,0:T(8,128)(2,1)S(1)}, u32[]{:S(2)}) copy-start(bf16[224,4096]{1,0:T(8,128)(2,1)S(1)} %collective-permute-done.5) | copy-start | bytes 5505028
  71.8 30.7 %copy-start.4 = (bf16[768,4096]{1,0:T(8,128)(2,1)}, bf16[768,4096]{1,0:T(8,128)(2,1)S(1)}, u32[]{:S(2)}) copy-start(bf16[768,4096]{1,0:T(8,128)(2,1)S(1)} %slice_dynamic-update-slice_fusion.2.pair_ref.refs_0_) | copy-start | bytes 18874372
  72.5 18.2 %copy-start.35 = (s32[256]{0:T(256)}, s32[256]{0:T(256)S(1)}, u32[]{:S(2)}) copy-start(s32[256]{0:T(256)S(1)} %collective-permute-done.7) | copy-start | bytes 3076
  72.6 18.0 %copy-start.16 = (bf16[224,4096]{1,0:T(8,128)(2,1)}, bf16[224,4096]{1,0:T(8,128)(2,1)S(1)}, u32[]{:S(2)}) copy-start(bf16[224,4096]{1,0:T(8,128)(2,1)S(1)} %collective-permute-done.8) | copy-start | bytes 5505028
  72.6 18.3 %collective-permute-start.12 = (bf16[768,4096]{1,0:T(8,128)(2,1)S(1)}, bf16[768,4096]{1,0:T(8,128)(2,1)S(1)}, u32[]{:S(2)}, u32[]{:S(2)}) collective-permute-start(bf16[768,4096]{1,0:T(8,128)(2,1)S(1)} %slice_dynamic-update-slice_fusion.2.pair_ref.refs_0_), channel_id=1, source_target_pairs={{0,1},{1,0},{4,5},{5,4},{8,9},{9,8},{12,13},{13,12},{2,3},{3,2},{6... | collective-permute-start | bytes 18874376 | tf_op jit(solution)/shard_map/ppermute | solution.py:38
  72.7 14.3 %collective-permute-start.9 = (bf16[64,4096]{1,0:T(8,128)(2,1)S(1)}, bf16[64,4096]{1,0:T(8,128)(2,1)S(1)}, u32[]{:S(2)}, u32[]{:S(2)}) collective-permute-start(bf16[64,4096]{1,0:T(8,128)(2,1)S(1)} %pad_maximum_fusion.16), channel_id=1, source_target_pairs={{0,2},{1,3},{4,6},{5,7},{8,10},{9,11},{12,14},{13,15},{2,0},{3,1},... | collective-permute-start | bytes 1572872 | tf_op jit(solution)/shard_map/ppermute | solution.py:38
  74.2 16.7 %collective-permute-start.13 = (bf16[64,4096]{1,0:T(8,128)(2,1)S(1)}, bf16[64,4096]{1,0:T(8,128)(2,1)S(1)}, u32[]{:S(2)}, u32[]{:S(2)}) collective-permute-start(bf16[64,4096]{1,0:T(8,128)(2,1)S(1)} %pad_maximum_fusion.16), channel_id=1, source_target_pairs={{0,66},{1,67},{4,70},{5,71},{8,74},{9,75},{12,78},{13,79},{2,64},{... | collective-permute-start | bytes 1572872 | tf_op jit(solution)/shard_map/ppermute | solution.py:38
  75.6 14.9 %collective-permute-start.10 = (bf16[64,4096]{1,0:T(8,128)(2,1)S(1)}, bf16[64,4096]{1,0:T(8,128)(2,1)S(1)}, u32[]{:S(2)}, u32[]{:S(2)}) collective-permute-start(bf16[64,4096]{1,0:T(8,128)(2,1)S(1)} %slice.140), channel_id=1, source_target_pairs={{0,4},{1,5},{4,8},{5,9},{8,12},{9,13},{12,0},{13,1},{2,6},{3,7},{6... | collective-permute-start | bytes 1572872 | tf_op jit(solution)/shard_map/ppermute | solution.py:38
  75.6 14.9 %collective-permute-start.11 = (bf16[64,4096]{1,0:T(8,128)(2,1)S(1)}, bf16[64,4096]{1,0:T(8,128)(2,1)S(1)}, u32[]{:S(2)}, u32[]{:S(2)}) collective-permute-start(bf16[64,4096]{1,0:T(8,128)(2,1)S(1)} %slice.141), channel_id=1, source_target_pairs={{0,12},{1,13},{4,0},{5,1},{8,4},{9,5},{12,8},{13,9},{2,14},{3,15},... | collective-permute-start | bytes 1572872 | tf_op jit(solution)/shard_map/ppermute | solution.py:38
  78.9 16.8 %copy-start.8 = (bf16[1,336,4096]{2,1,0:T(8,128)(2,1)S(1)}, bf16[1,336,4096]{2,1,0:T(8,128)(2,1)}, u32[]{:S(2)}) copy-start(bf16[1,336,4096]{2,1,0:T(8,128)(2,1)} %param.13) | copy-start | bytes 8257540
  80.8 15.0 %copy-start.6 = (bf16[1,336,4096]{2,1,0:T(8,128)(2,1)S(1)}, bf16[1,336,4096]{2,1,0:T(8,128)(2,1)}, u32[]{:S(2)}) copy-start(bf16[1,336,4096]{2,1,0:T(8,128)(2,1)} %param.11) | copy-start | bytes 8257540
  80.8 15.0 %copy-start.7 = (bf16[1,336,4096]{2,1,0:T(8,128)(2,1)S(1)}, bf16[1,336,4096]{2,1,0:T(8,128)(2,1)}, u32[]{:S(2)}) copy-start(bf16[1,336,4096]{2,1,0:T(8,128)(2,1)} %param.12) | copy-start | bytes 8257540
  90.6 8.4 %copy-start.31 = (bf16[64,4096]{1,0:T(8,128)(2,1)}, bf16[64,4096]{1,0:T(8,128)(2,1)S(1)}, u32[]{:S(2)}) copy-start(bf16[64,4096]{1,0:T(8,128)(2,1)S(1)} %collective-permute-done.11) | copy-start | bytes 1572868
  90.8 8.2 %copy-start.2 = (bf16[256,4096]{1,0:T(8,128)(2,1)}, bf16[256,4096]{1,0:T(8,128)(2,1)S(1)}, u32[]{:S(2)}) copy-start(bf16[256,4096]{1,0:T(8,128)(2,1)S(1)} %pad_maximum_fusion.13.pair_ref.refs_2_) | copy-start | bytes 6291460
  90.8 8.2 %copy-start.29 = (bf16[64,4096]{1,0:T(8,128)(2,1)}, bf16[64,4096]{1,0:T(8,128)(2,1)S(1)}, u32[]{:S(2)}) copy-start(bf16[64,4096]{1,0:T(8,128)(2,1)S(1)} %collective-permute-done.13) | copy-start | bytes 1572868
  90.8 11.7 %copy-start.5 = (bf16[768,4096]{1,0:T(8,128)(2,1)}, bf16[768,4096]{1,0:T(8,128)(2,1)S(1)}, u32[]{:S(2)}) copy-start(bf16[768,4096]{1,0:T(8,128)(2,1)S(1)} %collective-permute-done.12.other_ref.refs_1_) | copy-start | bytes 18874372
  90.8 4.9 %collective-permute-start.14 = (bf16[256,4096]{1,0:T(8,128)(2,1)S(1)}, bf16[256,4096]{1,0:T(8,128)(2,1)S(1)}, u32[]{:S(2)}, u32[]{:S(2)}) collective-permute-start(bf16[256,4096]{1,0:T(8,128)(2,1)S(1)} %pad_maximum_fusion.13.pair_ref.refs_2_), channel_id=1, source_target_pairs={{0,1},{1,0},{4,5},{5,4},{8,9},{9,8},{12,13},{13,12},{2,3},{3,2},{6... | collective-permute-start | bytes 6291464 | tf_op jit(solution)/shard_map/ppermute | solution.py:38
  90.9 19.9 %collective-permute-start.18 = (bf16[64,4096]{1,0:T(8,128)(2,1)}, bf16[64,4096]{1,0:T(8,128)(2,1)}, u32[]{:S(2)}, u32[]{:S(2)}) collective-permute-start(bf16[64,4096]{1,0:T(8,128)(2,1)} %pad_maximum_fusion.17), channel_id=1, source_target_pairs={{0,12},{1,13},{4,0},{5,1},{8,4},{9,5},{12,8},{13,9},{2,14},{3,15},... | collective-permute-start | bytes 1572872 | tf_op jit(solution)/shard_map/ppermute | solution.py:38
  94.0 16.9 %collective-permute-start.17 = (bf16[64,4096]{1,0:T(8,128)(2,1)}, bf16[64,4096]{1,0:T(8,128)(2,1)}, u32[]{:S(2)}, u32[]{:S(2)}) collective-permute-start(bf16[64,4096]{1,0:T(8,128)(2,1)} %pad_maximum_fusion.17), channel_id=1, source_target_pairs={{0,4},{1,5},{4,8},{5,9},{8,12},{9,13},{12,0},{13,1},{2,6},{3,7},{6... | collective-permute-start | bytes 1572872 | tf_op jit(solution)/shard_map/ppermute | solution.py:38
  94.0 19.9 %collective-permute-start.15 = (bf16[96,4096]{1,0:T(8,128)(2,1)}, bf16[96,4096]{1,0:T(8,128)(2,1)}, u32[]{:S(2)}, u32[]{:S(2)}) collective-permute-start(bf16[96,4096]{1,0:T(8,128)(2,1)} %slice.110), channel_id=1, source_target_pairs={{0,2},{1,3},{4,6},{5,7},{8,10},{9,11},{12,14},{13,15},{2,0},{3,1},... | collective-permute-start | bytes 2359304 | tf_op jit(solution)/shard_map/ppermute | solution.py:38
  95.2 19.6 %collective-permute-start.16 = (bf16[96,4096]{1,0:T(8,128)(2,1)}, bf16[96,4096]{1,0:T(8,128)(2,1)}, u32[]{:S(2)}, u32[]{:S(2)}) collective-permute-start(bf16[96,4096]{1,0:T(8,128)(2,1)} %pad_maximum_fusion.15), channel_id=1, source_target_pairs={{0,66},{1,67},{4,70},{5,71},{8,74},{9,75},{12,78},{13,79},{2,64},{... | collective-permute-start | bytes 2359304 | tf_op jit(solution)/shard_map/ppermute | solution.py:38
  95.7 3.3 %copy-start.10 = (bf16[256,4096]{1,0:T(8,128)(2,1)}, bf16[256,4096]{1,0:T(8,128)(2,1)S(1)}, u32[]{:S(2)}) copy-start(bf16[256,4096]{1,0:T(8,128)(2,1)S(1)} %collective-permute-done.14.other_ref.refs_3_) | copy-start | bytes 6291460
  99.0 3.2 %copy-start.14 = (bf16[768,256]{1,0:T(8,128)(2,1)}, bf16[768,256]{1,0:T(8,128)(2,1)S(1)}, u32[]{:S(2)}) copy-start(bf16[768,256]{1,0:T(8,128)(2,1)S(1)} %get-tuple-element.112.grads_ref.refs_16_) | copy-start | bytes 1179652
  102.2 8.5 %copy-start.21 = (bf16[224,4096]{1,0:T(8,128)(2,1)S(1)}, bf16[224,4096]{1,0:T(8,128)(2,1)}, u32[]{:S(2)}) copy-start(bf16[224,4096]{1,0:T(8,128)(2,1)} %copy-done.19) | copy-start | bytes 5505028
  102.2 8.5 %copy-start.23 = (bf16[224,4096]{1,0:T(8,128)(2,1)S(1)}, bf16[224,4096]{1,0:T(8,128)(2,1)}, u32[]{:S(2)}) copy-start(bf16[224,4096]{1,0:T(8,128)(2,1)} %copy-done.22) | copy-start | bytes 5505028
  102.2 8.5 %copy-start.17 = (bf16[224,4096]{1,0:T(8,128)(2,1)S(1)}, bf16[224,4096]{1,0:T(8,128)(2,1)}, u32[]{:S(2)}) copy-start(bf16[224,4096]{1,0:T(8,128)(2,1)} %copy-done.16) | copy-start | bytes 5505028
  102.2 12.6 %collective-permute-start.19 = (bf16[128,4096]{1,0:T(8,128)(2,1)S(1)}, bf16[128,4096]{1,0:T(8,128)(2,1)S(1)}, u32[]{:S(2)}, u32[]{:S(2)}) collective-permute-start(bf16[128,4096]{1,0:T(8,128)(2,1)S(1)} %get-tuple-element.113), channel_id=1, source_target_pairs={{0,1},{1,0},{4,5},{5,4},{8,9},{9,8},{12,13},{13,12},{2,3},{3,2},{6... | collective-permute-start | bytes 3145736 | tf_op jit(solution)/shard_map/ppermute | solution.py:38
  110.7 11.7 %copy-start.12 = (bf16[768,768]{1,0:T(8,128)(2,1)}, bf16[768,768]{1,0:T(8,128)(2,1)S(1)}, u32[]{:S(2)}) copy-start(bf16[768,768]{1,0:T(8,128)(2,1)S(1)} %get-tuple-element.119.grads_ref.refs_15_) | copy-start | bytes 3538948
  122.4 12.0 %collective-permute-start.20 = (bf16[384,4096]{1,0:T(8,128)(2,1)S(1)}, bf16[384,4096]{1,0:T(8,128)(2,1)S(1)}, u32[]{:S(2)}, u32[]{:S(2)}) collective-permute-start(bf16[384,4096]{1,0:T(8,128)(2,1)S(1)} %get-tuple-element.121), channel_id=1, source_target_pairs={{0,1},{1,0},{4,5},{5,4},{8,9},{9,8},{12,13},{13,12},{2,3},{3,2},{6... | collective-permute-start | bytes 9437192 | tf_op jit(solution)/shard_map/ppermute | solution.py:38
  124.2 6.7 %copy-start.32 = (bf16[64,4096]{1,0:T(8,128)(2,1)S(1)}, bf16[64,4096]{1,0:T(8,128)(2,1)}, u32[]{:S(2)}) copy-start(bf16[64,4096]{1,0:T(8,128)(2,1)} %copy-done.31) | copy-start | bytes 1572868
  124.5 8.6 %copy-start.28 = (bf16[128,4096]{1,0:T(8,128)(2,1)S(1)}, bf16[128,4096]{1,0:T(8,128)(2,1)}, u32[]{:S(2)}) copy-start(bf16[128,4096]{1,0:T(8,128)(2,1)} %copy-done.27) | copy-start | bytes 3145732
  125.6 11.8 %collective-permute-start.21 = (bf16[32,4096]{1,0:T(8,128)(2,1)S(1)}, bf16[32,4096]{1,0:T(8,128)(2,1)S(1)}, u32[]{:S(2)}, u32[]{:S(2)}) collective-permute-start(bf16[32,4096]{1,0:T(8,128)(2,1)S(1)} %slice.115), channel_id=1, source_target_pairs={{0,4},{1,5},{4,8},{5,9},{8,12},{9,13},{12,0},{13,1},{2,6},{3,7},{6... | collective-permute-start | bytes 786440 | tf_op jit(solution)/shard_map/ppermute | solution.py:38
  125.7 11.7 %collective-permute-start.22 = (bf16[32,4096]{1,0:T(8,128)(2,1)S(1)}, bf16[32,4096]{1,0:T(8,128)(2,1)S(1)}, u32[]{:S(2)}, u32[]{:S(2)}) collective-permute-start(bf16[32,4096]{1,0:T(8,128)(2,1)S(1)} %slice.116), channel_id=1, source_target_pairs={{0,12},{1,13},{4,0},{5,1},{8,4},{9,5},{12,8},{13,9},{2,14},{3,15},... | collective-permute-start | bytes 786440 | tf_op jit(solution)/shard_map/ppermute | solution.py:38
  128.9 12.6 %collective-permute-start.23 = (bf16[64,4096]{1,0:T(8,128)(2,1)S(1)}, bf16[64,4096]{1,0:T(8,128)(2,1)S(1)}, u32[]{:S(2)}, u32[]{:S(2)}) collective-permute-start(bf16[64,4096]{1,0:T(8,128)(2,1)S(1)} %slice.114), channel_id=1, source_target_pairs={{0,2},{1,3},{4,6},{5,7},{8,10},{9,11},{12,14},{13,15},{2,0},{3,1},... | collective-permute-start | bytes 1572872 | tf_op jit(solution)/shard_map/ppermute | solution.py:38
  130.9 12.0 %collective-permute-start.24 = (bf16[64,4096]{1,0:T(8,128)(2,1)S(1)}, bf16[64,4096]{1,0:T(8,128)(2,1)S(1)}, u32[]{:S(2)}, u32[]{:S(2)}) collective-permute-start(bf16[64,4096]{1,0:T(8,128)(2,1)S(1)} %copy-done.32), channel_id=1, source_target_pairs={{0,66},{1,67},{4,70},{5,71},{8,74},{9,75},{12,78},{13,79},{2,64},{... | collective-permute-start | bytes 1572872 | tf_op jit(solution)/shard_map/ppermute | solution.py:38
  137.4 10.2 %copy-start.30 = (bf16[64,4096]{1,0:T(8,128)(2,1)S(1)}, bf16[64,4096]{1,0:T(8,128)(2,1)}, u32[]{:S(2)}) copy-start(bf16[64,4096]{1,0:T(8,128)(2,1)} %copy-done.29) | copy-start | bytes 1572868
  142.9 7.8 %copy-start.9 = (bf16[1,336,4096]{2,1,0:T(8,128)(2,1)S(1)}, bf16[1,336,4096]{2,1,0:T(8,128)(2,1)}, u32[]{:S(2)}) copy-start(bf16[1,336,4096]{2,1,0:T(8,128)(2,1)} %param.13) | copy-start | bytes 8257540
  142.9 23.0 %collective-permute-start.30 = (bf16[64,4096]{1,0:T(8,128)(2,1)}, bf16[64,4096]{1,0:T(8,128)(2,1)}, u32[]{:S(2)}, u32[]{:S(2)}) collective-permute-start(bf16[64,4096]{1,0:T(8,128)(2,1)} %get-tuple-element.145), channel_id=1, source_target_pairs={{0,2},{1,3},{4,6},{5,7},{8,10},{9,11},{12,14},{13,15},{2,0},{3,1},... | collective-permute-start | bytes 1572872 | tf_op jit(solution)/shard_map/ppermute | solution.py:38
  144.4 22.6 %collective-permute-start.28 = (bf16[128,4096]{1,0:T(8,128)(2,1)}, bf16[128,4096]{1,0:T(8,128)(2,1)}, u32[]{:S(2)}, u32[]{:S(2)}) collective-permute-start(bf16[128,4096]{1,0:T(8,128)(2,1)} %get-tuple-element.143), channel_id=1, source_target_pairs={{0,12},{1,13},{4,0},{5,1},{8,4},{9,5},{12,8},{13,9},{2,14},{3,15},... | collective-permute-start | bytes 3145736 | tf_op jit(solution)/shard_map/ppermute | solution.py:38
  146.0 23.4 %collective-permute-start.29 = (bf16[128,4096]{1,0:T(8,128)(2,1)}, bf16[128,4096]{1,0:T(8,128)(2,1)}, u32[]{:S(2)}, u32[]{:S(2)}) collective-permute-start(bf16[128,4096]{1,0:T(8,128)(2,1)} %get-tuple-element.144), channel_id=1, source_target_pairs={{0,4},{1,5},{4,8},{5,9},{8,12},{9,13},{12,0},{13,1},{2,6},{3,7},{6... | collective-permute-start | bytes 3145736 | tf_op jit(solution)/shard_map/ppermute | solution.py:38
  146.5 4.2 %collective-permute-start.26 = (bf16[256,4096]{1,0:T(8,128)(2,1)S(1)}, bf16[256,4096]{1,0:T(8,128)(2,1)S(1)}, u32[]{:S(2)}, u32[]{:S(2)}) collective-permute-start(bf16[256,4096]{1,0:T(8,128)(2,1)S(1)} %pad_maximum_fusion.14.pair_ref.refs_6_), channel_id=1, source_target_pairs={{0,1},{1,0},{4,5},{5,4},{8,9},{9,8},{12,13},{13,12},{2,3},{3,2},{6... | collective-permute-start | bytes 6291464 | tf_op jit(solution)/shard_map/ppermute | solution.py:38
  148.8 6.3 %collective-permute-start.27 = (bf16[384,4096]{1,0:T(8,128)(2,1)S(1)}, bf16[384,4096]{1,0:T(8,128)(2,1)S(1)}, u32[]{:S(2)}, u32[]{:S(2)}) collective-permute-start(bf16[384,4096]{1,0:T(8,128)(2,1)S(1)} %slice_dynamic-update-slice_fusion.5.pair_ref.refs_8_), channel_id=1, source_target_pairs={{0,1},{1,0},{4,5},{5,4},{8,9},{9,8},{12,13},{13,12},{2,3},{3,2},{6... | collective-permute-start | bytes 9437192 | tf_op jit(solution)/shard_map/ppermute | solution.py:38
  150.6 9.9 %collective-permute-start.25 = (bf16[384,4096]{1,0:T(8,128)(2,1)S(1)}, bf16[384,4096]{1,0:T(8,128)(2,1)S(1)}, u32[]{:S(2)}, u32[]{:S(2)}) collective-permute-start(bf16[384,4096]{1,0:T(8,128)(2,1)S(1)} %pad_maximum_fusion.pair_ref.refs_4_), channel_id=1, source_target_pairs={{0,1},{1,0},{4,5},{5,4},{8,9},{9,8},{12,13},{13,12},{2,3},{3,2},{6... | collective-permute-start | bytes 9437192 | tf_op jit(solution)/shard_map/ppermute | solution.py:38
  160.5 8.9 %copy-start.18 = (bf16[128,4096]{1,0:T(8,128)(2,1)S(1)}, bf16[128,4096]{1,0:T(8,128)(2,1)}, u32[]{:S(2)}) copy-start(bf16[128,4096]{1,0:T(8,128)(2,1)} %get-tuple-element.155) | copy-start | bytes 3145732
  169.4 4.0 %copy-start.13 = (bf16[768,768]{1,0:T(8,128)(2,1)S(1)}, bf16[768,768]{1,0:T(8,128)(2,1)}, u32[]{:S(2)}) copy-start(bf16[768,768]{1,0:T(8,128)(2,1)} %copy-done.12) | copy-start | bytes 3538948
  171.5 2.4 %copy-start.11 = (bf16[256,4096]{1,0:T(8,128)(2,1)S(1)}, bf16[256,4096]{1,0:T(8,128)(2,1)}, u32[]{:S(2)}) copy-start(bf16[256,4096]{1,0:T(8,128)(2,1)} %copy-done.10) | copy-start | bytes 6291460
  171.5 2.4 %copy-start.15 = (bf16[768,256]{1,0:T(8,128)(2,1)S(1)}, bf16[768,256]{1,0:T(8,128)(2,1)}, u32[]{:S(2)}) copy-start(bf16[768,256]{1,0:T(8,128)(2,1)} %copy-done.14) | copy-start | bytes 1179652
  173.0 13.6 %collective-permute-start.31 = (bf16[64,4096]{1,0:T(8,128)(2,1)S(1)}, bf16[64,4096]{1,0:T(8,128)(2,1)S(1)}, u32[]{:S(2)}, u32[]{:S(2)}) collective-permute-start(bf16[64,4096]{1,0:T(8,128)(2,1)S(1)} %slice.158), channel_id=1, source_target_pairs={{0,2},{1,3},{4,6},{5,7},{8,10},{9,11},{12,14},{13,15},{2,0},{3,1},... | collective-permute-start | bytes 1572872 | tf_op jit(solution)/shard_map/ppermute | solution.py:38
  173.4 13.2 %collective-permute-start.32 = (bf16[64,4096]{1,0:T(8,128)(2,1)S(1)}, bf16[64,4096]{1,0:T(8,128)(2,1)S(1)}, u32[]{:S(2)}, u32[]{:S(2)}) collective-permute-start(bf16[64,4096]{1,0:T(8,128)(2,1)S(1)} %add_convert_fusion.3), channel_id=1, source_target_pairs={{0,8},{1,9},{4,12},{5,13},{8,0},{9,1},{12,4},{13,5},{2,10},{3,11},... | collective-permute-start | bytes 1572872 | tf_op jit(solution)/shard_map/ppermute | solution.py:38
  186.8 14.8 %copy-start.34 = (s32[64]{0:T(128)S(1)}, s32[64]{0:T(128)}, u32[]{:S(2)}) copy-start(s32[64]{0:T(128)} %copy-done.33) | copy-start | bytes 772
  186.8 14.8 %copy-start.36 = (s32[256]{0:T(256)S(1)}, s32[256]{0:T(256)}, u32[]{:S(2)}) copy-start(s32[256]{0:T(256)} %copy-done.35) | copy-start | bytes 3076
  186.8 14.8 %collective-permute-start.33 = (bf16[64,4096]{1,0:T(8,128)(2,1)S(1)}, bf16[64,4096]{1,0:T(8,128)(2,1)S(1)}, u32[]{:S(2)}, u32[]{:S(2)}) collective-permute-start(bf16[64,4096]{1,0:T(8,128)(2,1)S(1)} %add_convert_fusion.2), channel_id=1, source_target_pairs={{16,0},{32,16},{48,32},{17,1},{33,17},{49,33},{18,2},{34,18},{50,3... | collective-permute-start | bytes 1572872 | tf_op jit(solution)/shard_map/ppermute | solution.py:318
  188.7 15.0 %copy-start.1 = (bf16[1,1,256,4096]{3,2,1,0:T(8,128)(2,1)S(1)}, bf16[1,1,256,4096]{3,2,1,0:T(8,128)(2,1)}, u32[]{:S(2)}) copy-start(bf16[1,1,256,4096]{3,2,1,0:T(8,128)(2,1)} %param.7) | copy-start | bytes 6291460
  (11 other events, 17.3 us)
where the time goes:
time: 206 us; the launch traced here: 204 us
  waiting for transfers between devices  74.3 us (36%)
  Pallas kernels  60.6 us (29%)
  starting transfers between devices  38.1 us (18%)
  local copies, waits for them, and re-layouts  13.3 us (6%)
  other arithmetic  11.1 us (5%)
  matrix products  4.81 us (2%)
    ppermute x32, waiting for transfers between devices, send(): return lax.ppermute(value, AXES, pairs)  74.3 us
    ppermute x32, starting transfers between devices, send(): return lax.ppermute(value, AXES, pairs)  33.8 us
    pallas_call x2, Pallas kernels, weight_grads(): pl.pallas_call(kernel, grid=(count,), in_specs=[hbm] * n + whole + [hbm]...  25.5 us
    pallas_call x5, Pallas kernels, forward(): pl.pallas_call(kernel, in_specs=[ON_CHIP] * 5, out_specs=[ON_CHIP] * 2, o...  25.4 us
    pallas_call x2, Pallas kernels, input_terms(): pl.pallas_call(kernel, in_specs=[ON_CHIP] * 3, out_specs=[ON_CHIP] * 2, o...  9.72 us
    concatenate x7, other arithmetic, join(): return jnp.concatenate(parts, axis=0)  4.98 us
    dot_general x3, matrix products, matmul(): return jnp.dot(left, right, preferred_element_type=jnp.float32)  4.81 us
    unnamed x89, local copies, waits for them, and re-layouts  4.64 us
  transfers between devices with their start and end apart: 34, of which 17 were waited for; matrix products, arithmetic and copies ran while one was open for 7% of the time, Pallas kernels for 27%

commit v1 on v0

--- a/solution.py
+++ b/solution.py
@@ -66,13 +66,16 @@
     return v.astype(jnp.float32)
 
 
-SMALL = pl.CostEstimate(flops=1 << 36, bytes_accessed=1 << 30, transcendentals=0)
 GAP = 384
 FWD, TERM, SUMS = 14, 10, 24
 ON_CHIP = pl.BlockSpec(memory_space=pltpu.VMEM)
 
 
-def forward(pair, other, gate, up, down):
+def cost(effort):
+    return pl.CostEstimate(flops=effort, bytes_accessed=1 << 16, transcendentals=0)
+
+
+def forward(pair, other, gate, up, down, effort):
     tile = 1024
     m, (units, width) = pair.shape[0] // 2, gate.shape
 
@@ -110,11 +113,11 @@
         ],
         scratch_shapes=[pltpu.VMEM((3, units, 2 * m), jnp.float32)],
         compiler_params=pltpu.CompilerParams(vmem_limit_bytes=FWD << 20),
-        cost_estimate=SMALL,
+        cost_estimate=cost(effort),
     )(pair, other, gate, up, down)
 
 
-def input_terms(grads, gate, up):
+def input_terms(grads, gate, up, effort):
     tile = 512
     n, (units, width) = grads.shape[1], gate.shape
     m = n // 2
@@ -142,11 +145,11 @@
             pltpu.VMEM((2 * GAP, tile), jnp.bfloat16),
         ],
         compiler_params=pltpu.CompilerParams(vmem_limit_bytes=TERM << 20),
-        cost_estimate=SMALL,
+        cost_estimate=cost(effort),
     )(grads, gate, up)
 
 
-def weight_grads(pairs, hiddens, grads, first, count, earlier):
+def weight_grads(pairs, hiddens, grads, first, count, earlier, effort):
     tile = 512
     n = len(pairs)
     units, width = hiddens[0].shape[0], pairs[0].shape[1]
@@ -183,7 +186,8 @@
             for k in range(n // 2):
                 m = hidden_refs[k].shape[1]
                 hidden[:, start : start + m] = hidden_refs[k][...]
-                grad[:, start : start + m] = grads_refs[k][...]
+                grad[:units, start : start + m] = grads_refs[k][:units, :]
+                grad[units:, start : start + m] = grads_refs[k][GAP : GAP + units, :]
                 start += m
 
         slot = lax.rem(step, 2)
@@ -195,9 +199,9 @@
 
         for c in copies(step, slot):
             c.wait()
-        right = acts[slot]
-        gate_out[...] = half(matmul(grad[:units, :], right))
-        up_out[...] = half(matmul(grad[GAP : GAP + units, :], right))
+        both = half(matmul(grad[...], acts[slot]))
+        gate_out[...] = both[:units]
+        up_out[...] = both[units:]
         down_out[...] = half(matmul(hidden[...], rows_grads[slot]))
 
     whole = [
@@ -215,11 +219,11 @@
             pltpu.VMEM((2, total, tile), jnp.bfloat16),
             pltpu.VMEM((2, total, tile), jnp.bfloat16),
             pltpu.VMEM((units, total), jnp.bfloat16),
-            pltpu.VMEM((2 * GAP, total), jnp.bfloat16),
+            pltpu.VMEM((2 * units, total), jnp.bfloat16),
             pltpu.SemaphoreType.DMA((2, 2 * n)),
         ],
         compiler_params=pltpu.CompilerParams(vmem_limit_bytes=SUMS << 20),
-        cost_estimate=SMALL,
+        cost_estimate=cost(effort),
     )(*pairs, *hiddens, *grads, *earlier)
 
 
@@ -264,48 +268,52 @@
         a, a_is, from_b[32:160], from_u[32:160],
         g, from_i[32:96], g_sb, from_i[96:160], g_su, from_i[160:224],
     )
+    x1_pair = join(a_os, from_b[160:224], from_u[160:224], from_o[32:224])
     a_ts, g_st = join(from_i[:32], from_o[:32]), join(from_b[:32], from_u[:32])
-    own_pair, g_st, a_sb, a_iu, next_slot, from_i, from_o, from_b, from_u = together(
-        own_pair, g_st, from_b[32:96], from_u[96:160], next_slot, from_i, from_o, from_b, from_u
-    )
-    g_it, g_ot, a_st, a_it = send(g_st, INNER), send(g_st, OUTER), send(a_sb, UP), send(a_iu, DOWN)
+    to_i, to_o, to_u, to_b, own_pair, a_ts, g_st, next_slot = together(
+        join(g_st, from_o[32:128]),
+        join(g_st, from_i[128:224]),
+        join(from_b[32:96], a_ts, from_b[160:192]),
+        join(from_u[96:160], a_ts, from_u[192:224]),
+        own_pair, a_ts, g_st, next_slot,
+    )
+    more_i, more_o, more_b, more_u = send(to_i, INNER), send(to_o, OUTER), send(to_u, UP), send(to_b, DOWN)
     own_other = send(own_pair, SIBLING)
-    far_pair = join(a_st, a_it, g_st, g_it)
-    to_i, to_o, a_ts, far_pair, own_pair, own_other, g_ot, a_it, from_o, from_b, from_u = together(
-        from_o[96:192], join(from_i[192:224], g_it), a_ts, far_pair, own_pair, own_other, g_ot, a_it,
-        from_o, from_b, from_u,
-    )
+    hidden_own, grads_own = forward(own_pair, own_other, *weights, 1 << 20)
+    term_own, term_own2 = input_terms(grads_own, gate_local, up_local, 1 << 36)
+    term_own, term_own2, more_i, more_o, more_b, more_u = together(
+        term_own, term_own2, more_i, more_o, more_b, more_u
+    )
+    far_pair = join(more_b[:64], more_u[:64], g_st, more_i[:64])
+    to_o = join(more_u[:64], more_i[:64])
     far_other = send(far_pair, SIBLING)
-    g_i, g_o, a_tb, a_tu = send(to_i, INNER), send(to_o, OUTER), send(a_ts, UP), send(a_ts, DOWN)
-    hidden_far, grads_far = forward(far_pair, far_other, *weights)
-    term_far, term_far2 = input_terms(grads_far, gate_local, up_local)
+    term_from = send(term_own2, SIBLING)
+    hidden_far, grads_far = forward(far_pair, far_other, *weights, 1 << 20)
+    term_far, term_far2 = input_terms(grads_far, gate_local, up_local, 1 << 36)
+    term_far2, term_from = together(term_far2, term_from)
     far_from = send(term_far2, SIBLING)
-    hidden_own, grads_own = forward(own_pair, own_other, *weights)
-    g_i, g_o, a_tb, a_tu, far_from, grads_own, to_i, to_o, to_u, to_b = together(
-        g_i, g_o, a_tb, a_tu, far_from, grads_own, from_o[32:96], a_it, from_b[160:192], from_u[192:224]
-    )
-    g_ts, a_tt, a_ot1, a_ot2 = send(to_i, INNER), send(to_o, OUTER), send(to_u, UP), send(to_b, DOWN)
-    term_own, term_own2 = input_terms(grads_own, gate_local, up_local)
-    term_from = send(term_own2, SIBLING)
+    own = half(full(term_own) + full(term_from))
     far = half(full(term_far) + full(far_from))
-    own = half(full(term_own) + full(term_from))
-    x1_pair = join(a_os, from_b[160:224], from_u[160:224], from_o[32:224])
-    x2_pair = join(a_tb, a_tu, g_i, g_o[:32])
-    to_b, to_u, to_i, own0, far0, a_ot1, a_ot2, a_ts, g_ot, g_ts, a_tt, x1_pair, x2_pair = together(
-        own[128:256], own[256:384], far[64:128], own[:128], far[:64],
-        a_ot1, a_ot2, a_ts, g_ot, g_ts, a_tt, x1_pair, x2_pair,
-    )
-    z_u, z_b, far_i = send(to_b, DOWN), send(to_u, UP), send(to_i, INNER)
-    x3_pair = join(a_ot1, a_ot2, a_ts, a_tt, g_ot, g_ts, g_o[32:])
-    x1_other, x2_other, x3_other = send(x1_pair, SIBLING), send(x2_pair, SIBLING), send(x3_pair, SIBLING)
-    hidden_x1, grads_x1 = forward(x1_pair, x1_other, *weights)
-    hidden_x2, grads_x2 = forward(x2_pair, x2_other, *weights)
-    hidden_x3, grads_x3 = forward(x3_pair, x3_other, *weights)
-    z_u, z_b, far_i, hidden_x1, hidden_x2, hidden_x3 = together(
-        z_u, z_b, far_i, hidden_x1, hidden_x2, hidden_x3
-    )
+    to_b, to_u, to_i, own0, far0, to_o, more_i, more_o, more_b, more_u, x1_pair = together(
+        own[128:256], own[256:384], far[64:128], own[:128], far[:64], to_o,
+        more_i, more_o, more_b, more_u, x1_pair,
+    )
+    z_u, z_b, far_i, tt = send(to_b, DOWN), send(to_u, UP), send(to_i, INNER), send(to_o, OUTER)
+    x1_other = send(x1_pair, SIBLING)
+    x2_pair = join(
+        more_b[64:160], more_u[128:160], more_u[64:128], a_ts,
+        more_i[128:160], more_o[64:96], more_o[:64], more_o[96:160], more_i[64:128],
+    )
+    x2_other = send(x2_pair, SIBLING)
+    hidden_x1, grads_x1 = forward(x1_pair, x1_other, *weights, 1 << 36)
+    hidden_x2, grads_x2 = forward(x2_pair, x2_other, *weights, 1 << 36)
+    z_u, z_b, far_i, hidden_x1, hidden_x2 = together(z_u, z_b, far_i, hidden_x1, hidden_x2)
     near = full(own0) + full(z_u) + full(z_b)
-    to_i, to_t, near_s = together(half(near[64:]), half(full(far0) + full(far_i)), near[:64])
+    to_i, to_t, near_s, x3_pair = together(
+        half(near[64:]), half(full(far0) + full(far_i)), near[:64], tt
+    )
+    x3_other = send(x3_pair, SIBLING)
+    hidden_x3, grads_x3 = forward(x3_pair, x3_other, *weights, 1 << 36)
     near_i, far_t = send(to_i, INNER), send(to_t, ACROSS)
     pairs = [
         own_pair, own_other, far_pair, far_other,
@@ -313,11 +321,12 @@
     ]
     hiddens = [hidden_own, hidden_far, hidden_x1, hidden_x2, hidden_x3]
     grads = [grads_own, grads_far, grads_x1, grads_x2, grads_x3]
-    early = weight_grads(pairs, hiddens, grads, 0, 4, ())
-    input_rows, early = together(half(near_s + full(near_i) + full(far_t)), tuple(early))
+    early = weight_grads(pairs, hiddens, grads, 0, 4, (), 1 << 36)
+    near_i, far_t, near_s, early = together(near_i, far_t, near_s, tuple(early))
+    input_rows = half(near_s + full(near_i) + full(far_t))
     shifted = lax.ppermute(input_rows, "section", [(1, 0), (2, 1), (3, 2)])
     placer = half(next_slot[:, None] == wanted[None, :])
-    grad_gate, grad_up, grad_down = weight_grads(pairs, hiddens, grads, 4, 4, early)
+    grad_gate, grad_up, grad_down = weight_grads(pairs, hiddens, grads, 4, 4, early, 1 << 36)
     prev_grad = half(matmul(placer, shifted))[None, None]
     return (grad_gate[None], grad_up[None], grad_down[None], prev_grad)
 

time: 206 us -> 192 us (0.932)
  starting transfers between devices: 38.1 us -> 32.8 us
  local copies, waits for them, and re-layouts: 13.3 us -> 8.9 us
  other arithmetic: 11.1 us -> 7.32 us
  waiting for transfers between devices: 74.3 us -> 77.1 us
    ppermute x32 -> x25, starting transfers between devices: 33.8 us -> 28.1 us  [send(): return lax.ppermute(value, AXES, pairs)]
    ppermute x32 -> x25, waiting for transfers between devices: 74.3 us -> 77.1 us  [send(): return lax.ppermute(value, AXES, pairs)]
    slice x9 -> x5, local copies, waits for them, and re-layouts: 2.88 us -> 0.21 us  [the longest x3 0.11 us: per_device(): far_pair = join(more_b[:64], more_u[:64], g_st, more_i[:64])]
    unnamed x89 -> x79, local copies, waits for them, and re-layouts: 4.64 us -> 6.78 us
    concatenate x7 -> x8, other arithmetic: 4.98 us -> 4.12 us  [join(): return jnp.concatenate(parts, axis=0)]
  transfers between devices with their start and end apart: 34 -> 27, of which waited for: 17 -> 15; matrix products, arithmetic and copies ran while one was open for 7% -> 4% of each run, Pallas kernels for 27% -> 32%
where the time goes in v1:
time: 192 us; the launch traced here: 191 us
  waiting for transfers between devices  77.1 us (40%)
  Pallas kernels  60.5 us (32%)
  starting transfers between devices  32.8 us (17%)
  local copies, waits for them, and re-layouts  8.9 us (5%)
  other arithmetic  7.32 us (4%)
  matrix products  3.22 us (2%)
    ppermute x25, waiting for transfers between devices, send(): return lax.ppermute(value, AXES, pairs)  77.1 us
    ppermute x25, starting transfers between devices, send(): return lax.ppermute(value, AXES, pairs)  28.1 us
    pallas_call x5, Pallas kernels, forward(): pl.pallas_call(kernel, in_specs=[ON_CHIP] * 5, out_specs=[ON_CHIP] * 2, o...  25.4 us
    pallas_call x2, Pallas kernels, weight_grads(): pl.pallas_call(kernel, grid=(count,), in_specs=[hbm] * n + whole + [hbm]...  25.4 us
    pallas_call x2, Pallas kernels, input_terms(): pl.pallas_call(kernel, in_specs=[ON_CHIP] * 3, out_specs=[ON_CHIP] * 2, o...  9.71 us
    unnamed x79, local copies, waits for them, and re-layouts  6.78 us
    concatenate x8, other arithmetic, join(): return jnp.concatenate(parts, axis=0)  4.12 us
  transfers between devices with their start and end apart: 27, of which 15 were waited for; matrix products, arithmetic and copies ran while one was open for 4% of the time, Pallas kernels for 32%

profile of v1, /device:TPU:12, one launch (start us, length us, event | category | flops | bytes accessed | tf_op | source)
XLA Modules:
  0.0 191.3 jit_solution(140775051853274771)
XLA Ops:
  0.7 0.9 select_reduce_fusion.1
  1.7 0.6 copy-done
  2.3 0.5 convolution_convert_fusion.2
  2.8 0.5 copy-done.18
  3.3 0.6 convolution_convert_fusion.1
  3.9 0.6 collective-permute-start
  4.6 1.1 collective-permute-start.3
  5.7 1.9 %collective-permute-start.1 = (bf16[64,4096]{1,0:T(8,128)(2,1)S(1)}, bf16[64,4096]{1,0:T(8,128)(2,1)S(1)}, u32[]{:S(2)}, u32[]{:S(2)}) collective-permute-start(bf16[64,4096]{1,0:T(8,128)(2,1)S(1)} %convolution_convert_fusion.1), channel_id=1, source_target_pairs={{0,4},{1,5},{4,8},{5,9},{8,12},{9,13},{12,0},{13,1},{2,6},{3,7},{6... | collective-permute-start | bytes 1572872 | tf_op jit(solution)/shard_map/ppermute | solution.py:38
  7.6 2.1 %collective-permute-start.2 = (bf16[64,4096]{1,0:T(8,128)(2,1)S(1)}, bf16[64,4096]{1,0:T(8,128)(2,1)S(1)}, u32[]{:S(2)}, u32[]{:S(2)}) collective-permute-start(bf16[64,4096]{1,0:T(8,128)(2,1)S(1)} %convolution_convert_fusion.1), channel_id=1, source_target_pairs={{0,12},{1,13},{4,0},{5,1},{8,4},{9,5},{12,8},{13,9},{2,14},{3,15},... | collective-permute-start | bytes 1572872 | tf_op jit(solution)/shard_map/ppermute | solution.py:38
  9.7 7.9 %collective-permute-done = bf16[64,4096]{1,0:T(8,128)(2,1)S(1)} collective-permute-done((bf16[64,4096]{1,0:T(8,128)(2,1)S(1)}, bf16[64,4096]{1,0:T(8,128)(2,1)S(1)}, u32[]{:S(2)}, u32[]{:S(2)}) %collective-permute-start) | collective-permute-done | bytes 524320 | tf_op jit(solution)/shard_map/ppermute | solution.py:38
  18.0 3.1 %collective-permute-done.1 = bf16[64,4096]{1,0:T(8,128)(2,1)S(1)} collective-permute-done((bf16[64,4096]{1,0:T(8,128)(2,1)S(1)}, bf16[64,4096]{1,0:T(8,128)(2,1)S(1)}, u32[]{:S(2)}, u32[]{:S(2)}) %collective-permute-start.1) | collective-permute-done | bytes 524320 | tf_op jit(solution)/shard_map/ppermute | solution.py:38
  21.2 1.0 pad_maximum_fusion.1
  22.2 1.3 collective-permute-start.4
  23.5 2.0 %collective-permute-start.5 = (bf16[224,4096]{1,0:T(8,128)(2,1)S(1)}, bf16[224,4096]{1,0:T(8,128)(2,1)S(1)}, u32[]{:S(2)}, u32[]{:S(2)}) collective-permute-start(bf16[224,4096]{1,0:T(8,128)(2,1)S(1)} %get-tuple-element.78), channel_id=1, source_target_pairs={{0,12},{1,13},{4,0},{5,1},{8,4},{9,5},{12,8},{13,9},{2,14},{3,15},... | collective-permute-start | bytes 5505032 | tf_op jit(solution)/shard_map/ppermute | solution.py:38
  25.5 0.9 collective-permute-start.7
  26.4 1.6 collective-permute-start.6
  28.0 2.3 %collective-permute-start.8 = (s32[256]{0:T(256)S(1)}, s32[256]{0:T(256)S(1)}, u32[]{:S(2)}, u32[]{:S(2)}) collective-permute-start(s32[256]{0:T(256)S(1)} %broadcast_select_fusion), channel_id=1, source_target_pairs={{16,0},{32,16},{48,32},{17,1},{33,17},{49,33},{18,2},{34,18},{50,3... | collective-permute-start | bytes 3080 | tf_op jit(solution)/shard_map/ppermute | solution.py:266
  30.4 33.7 %collective-permute-done.4 = bf16[224,4096]{1,0:T(8,128)(2,1)S(1)} collective-permute-done((bf16[224,4096]{1,0:T(8,128)(2,1)S(1)}, bf16[224,4096]{1,0:T(8,128)(2,1)S(1)}, u32[]{:S(2)}, u32[]{:S(2)}) %collective-permute-start.4) | collective-permute-done | bytes 1835040 | tf_op jit(solution)/shard_map/ppermute | solution.py:38
  64.3 1.9 collective-permute-done.6
  66.4 0.3 pad_maximum_fusion.20
  66.9 0.4 fusion.7
  67.5 0.8 pad_maximum_fusion.22
  68.4 2.4 %collective-permute-start.10 = (bf16[160,4096]{1,0:T(8,128)(2,1)S(1)}, bf16[160,4096]{1,0:T(8,128)(2,1)S(1)}, u32[]{:S(2)}, u32[]{:S(2)}) collective-permute-start(bf16[160,4096]{1,0:T(8,128)(2,1)S(1)} %get-tuple-element.88), channel_id=1, source_target_pairs={{0,2},{1,3},{4,6},{5,7},{8,10},{9,11},{12,14},{13,15},{2,0},{3,1},... | collective-permute-start | bytes 3932168 | tf_op jit(solution)/shard_map/ppermute | solution.py:38
  70.8 2.1 %collective-permute-start.11 = (bf16[160,4096]{1,0:T(8,128)(2,1)S(1)}, bf16[160,4096]{1,0:T(8,128)(2,1)S(1)}, u32[]{:S(2)}, u32[]{:S(2)}) collective-permute-start(bf16[160,4096]{1,0:T(8,128)(2,1)S(1)} %get-tuple-element.89), channel_id=1, source_target_pairs={{0,66},{1,67},{4,70},{5,71},{8,74},{9,75},{12,78},{13,79},{2,64},{... | collective-permute-start | bytes 3932168 | tf_op jit(solution)/shard_map/ppermute | solution.py:38
  73.0 3.2 %collective-permute-start.13 = (bf16[160,4096]{1,0:T(8,128)(2,1)S(1)}, bf16[160,4096]{1,0:T(8,128)(2,1)S(1)}, u32[]{:S(2)}, u32[]{:S(2)}) collective-permute-start(bf16[160,4096]{1,0:T(8,128)(2,1)S(1)} %get-tuple-element.91), channel_id=1, source_target_pairs={{0,12},{1,13},{4,0},{5,1},{8,4},{9,5},{12,8},{13,9},{2,14},{3,15},... | collective-permute-start | bytes 3932168 | tf_op jit(solution)/shard_map/ppermute | solution.py:38
  76.2 2.3 %collective-permute-done.9.other_ref.refs_1_ = bf16[768,4096]{1,0:T(8,128)(2,1)S(1)} collective-permute-done((bf16[768,4096]{1,0:T(8,128)(2,1)S(1)}, bf16[768,4096]{1,0:T(8,128)(2,1)S(1)}, u32[]{:S(2)}, u32[]{:S(2)}) %collective-permute-start.9) | collective-permute-done | bytes 6291488 | tf_op jit(solution)/shard_map/ppermute | solution.py:38
  78.5 8.1 %shard_map.102 = (bf16[336,768]{1,0:T(8,128)(2,1)S(1)}, bf16[768,768]{1,0:T(8,128)(2,1)S(1)}) custom-call(bf16[768,4096]{1,0:T(8,128)(2,1)S(1)} %slice_dynamic-update-slice_fusion.3.pair_ref.refs_0_, bf16[768,4096]{1,0:T(8,128)(2,1)S(1)} %collective-permute-done.9.other_ref.refs_1_, bf16[336,4096]{1,0:T(8,128)(2,1)S(1)} %bitcast.18, ...), custom_call_target="tpu_custom_call" | custom-call | flops 1048576 | bytes 65536 | tf_op jit(solution)/shard_map/pallas_call | solution.py:106
  86.6 6.5 %shard_map.103 = (bf16[384,4096]{1,0:T(8,128)(2,1)S(1)}, bf16[384,4096]{1,0:T(8,128)(2,1)S(1)}) custom-call(bf16[768,768]{1,0:T(8,128)(2,1)S(1)} %get-tuple-element.85.grads_ref.refs_15_, bf16[336,4096]{1,0:T(8,128)(2,1)S(1)} %bitcast.19, bf16[336,4096]{1,0:T(8,128)(2,1)S(1)} %bitcast.26), custom_call_target="tpu_custom_call" | custom-call | flops 68719476736 | bytes 65536 | tf_op jit(solution)/shard_map/pallas_call | solution.py:138
  93.2 7.0 %collective-permute-done.10 = bf16[160,4096]{1,0:T(8,128)(2,1)S(1)} collective-permute-done((bf16[160,4096]{1,0:T(8,128)(2,1)S(1)}, bf16[160,4096]{1,0:T(8,128)(2,1)S(1)}, u32[]{:S(2)}, u32[]{:S(2)}) %collective-permute-start.10) | collective-permute-done | bytes 1310752 | tf_op jit(solution)/shard_map/ppermute | solution.py:38
  100.2 1.9 collective-permute-done.11
  102.0 2.7 %collective-permute-done.12 = bf16[160,4096]{1,0:T(8,128)(2,1)S(1)} collective-permute-done((bf16[160,4096]{1,0:T(8,128)(2,1)S(1)}, bf16[160,4096]{1,0:T(8,128)(2,1)S(1)}, u32[]{:S(2)}, u32[]{:S(2)}) %collective-permute-start.12) | collective-permute-done | bytes 1310752 | tf_op jit(solution)/shard_map/ppermute | solution.py:38
  104.8 1.0 copy-done.22
  105.8 0.4 copy-done.24
  106.6 0.3 pad_maximum_fusion.pair_ref.refs_4_
  107.0 0.8 collective-permute-start.15
  107.7 1.1 pad_maximum_fusion.21
  108.8 1.9 collective-permute-done.14.other_ref.refs_3_
  110.7 3.2 %shard_map.104 = (bf16[336,256]{1,0:T(8,128)(2,1)S(1)}, bf16[768,256]{1,0:T(8,128)(2,1)S(1)}) custom-call(bf16[256,4096]{1,0:T(8,128)(2,1)S(1)} %pad_maximum_fusion.13.pair_ref.refs_2_, bf16[256,4096]{1,0:T(8,128)(2,1)S(1)} %collective-permute-done.14.other_ref.refs_3_, bf16[336,4096]{1,0:T(8,128)(2,1)S(1)} %bitcast.20, bf16[336,4096]{1,0:T(8,128)(2,1)S(1)} %bitcast.27, ...), custom_call_target="tpu_custom_call" | custom-call | flops 1048576 | bytes 65536 | tf_op jit(solution)/shard_map/pallas_call | solution.py:106
  114.0 3.2 %shard_map.105 = (bf16[128,4096]{1,0:T(8,128)(2,1)S(1)}, bf16[128,4096]{1,0:T(8,128)(2,1)S(1)}) custom-call(bf16[768,256]{1,0:T(8,128)(2,1)S(1)} %get-tuple-element.97.grads_ref.refs_16_, bf16[336,4096]{1,0:T(8,128)(2,1)S(1)} %bitcast.21, bf16[336,4096]{1,0:T(8,128)(2,1)S(1)} %bitcast.28), custom_call_target="tpu_custom_call" | custom-call | flops 68719476736 | bytes 65536 | tf_op jit(solution)/shard_map/pallas_call | solution.py:138
  117.4 1.2 add_convert_fusion
  118.6 1.3 fusion.18
  119.9 0.2 add_convert_fusion.1
  120.3 0.9 copy-done.23
  121.2 0.3 copy-done.25
  121.7 0.4 collective-permute-start.17
  122.4 0.4 collective-permute-start.18
  122.8 2.5 %collective-permute-start.19 = (bf16[128,4096]{1,0:T(8,128)(2,1)}, bf16[128,4096]{1,0:T(8,128)(2,1)S(1)}, u32[]{:S(2)}, u32[]{:S(2)}) collective-permute-start(bf16[128,4096]{1,0:T(8,128)(2,1)} %get-tuple-element.111), channel_id=1, source_target_pairs={{0,12},{1,13},{4,0},{5,1},{8,4},{9,5},{12,8},{13,9},{2,14},{3,15},... | collective-permute-start | bytes 3145736 | tf_op jit(solution)/shard_map/ppermute | solution.py:38
  125.3 0.9 collective-permute-start.21
  126.2 1.2 collective-permute-done.17.other_ref.refs_5_
  127.4 0.3 collective-permute-start.22
  127.7 5.5 %shard_map.106 = (bf16[336,384]{1,0:T(8,128)(2,1)S(1)}, bf16[768,384]{1,0:T(8,128)(2,1)S(1)}) custom-call(bf16[384,4096]{1,0:T(8,128)(2,1)S(1)} %pad_maximum_fusion.pair_ref.refs_4_, bf16[384,4096]{1,0:T(8,128)(2,1)S(1)} %collective-permute-done.17.other_ref.refs_5_, bf16[336,4096]{1,0:T(8,128)(2,1)S(1)} %bitcast.22, bf16[336,4096]{1,0:T(8,128)(2,1)S(1)} %bitcast.29, ...), custom_call_target="tpu_custom_call" | custom-call | flops 68719476736 | bytes 65536 | tf_op jit(solution)/shard_map/pallas_call | solution.py:106
  133.4 5.6 %shard_map.107 = (bf16[336,512]{1,0:T(8,128)(2,1)S(1)}, bf16[768,512]{1,0:T(8,128)(2,1)S(1)}) custom-call(bf16[512,4096]{1,0:T(8,128)(2,1)S(1)} %slice_dynamic-update-slice_fusion.6.pair_ref.refs_6_, bf16[512,4096]{1,0:T(8,128)(2,1)S(1)} %collective-permute-done.18.other_ref.refs_7_, bf16[336,4096]{1,0:T(8,128)(2,1)S(1)} %bitcast.23, ...), custom_call_target="tpu_custom_call" | custom-call | flops 68719476736 | bytes 65536 | tf_op jit(solution)/shard_map/pallas_call | solution.py:106
  139.0 9.3 %collective-permute-done.19 = bf16[128,4096]{1,0:T(8,128)(2,1)S(1)} collective-permute-done((bf16[128,4096]{1,0:T(8,128)(2,1)}, bf16[128,4096]{1,0:T(8,128)(2,1)S(1)}, u32[]{:S(2)}, u32[]{:S(2)}) %collective-permute-start.19) | collective-permute-done | bytes 1048608 | tf_op jit(solution)/shard_map/ppermute | solution.py:38
  148.4 3.1 %collective-permute-done.20 = bf16[128,4096]{1,0:T(8,128)(2,1)S(1)} collective-permute-done((bf16[128,4096]{1,0:T(8,128)(2,1)S(1)}, bf16[128,4096]{1,0:T(8,128)(2,1)S(1)}, u32[]{:S(2)}, u32[]{:S(2)}) %collective-permute-start.20) | collective-permute-done | bytes 1048608 | tf_op jit(solution)/shard_map/ppermute | solution.py:38
  151.5 0.4 convert_add_fusion
  152.2 0.7 collective-permute-done.22.pair_ref.refs_8_
  152.8 2.1 %collective-permute-start.24 = (bf16[64,4096]{1,0:T(8,128)(2,1)S(1)}, bf16[64,4096]{1,0:T(8,128)(2,1)S(1)}, u32[]{:S(2)}, u32[]{:S(2)}) collective-permute-start(bf16[64,4096]{1,0:T(8,128)(2,1)S(1)} %slice.206), channel_id=1, source_target_pairs={{0,2},{1,3},{4,6},{5,7},{8,10},{9,11},{12,14},{13,15},{2,0},{3,1},... | collective-permute-start | bytes 1572872 | tf_op jit(solution)/shard_map/ppermute | solution.py:38
  154.9 1.0 collective-permute-start.25
  155.9 3.0 %shard_map.108 = (bf16[336,128]{1,0:T(8,128)(2,1)S(1)}, bf16[768,128]{1,0:T(8,128)(2,1)S(1)}) custom-call(bf16[128,4096]{1,0:T(8,128)(2,1)S(1)} %collective-permute-done.22.pair_ref.refs_8_, bf16[128,4096]{1,0:T(8,128)(2,1)S(1)} %collective-permute-done.23.other_ref.refs_9_, bf16[336,4096]{1,0:T(8,128)(2,1)S(1)} %bitcast.24, bf16[336,4096]{1,0:T(8,128)(2,1)S(1)} %bitcast.31, ...), custom_call_target="tpu_custom_call" | custom-call | flops 68719476736 | bytes 65536 | tf_op jit(solution)/shard_map/pallas_call | solution.py:106
  159.0 12.7 %shard_map.109 = (bf16[336,4096]{1,0:T(8,128)(2,1)}, bf16[336,4096]{1,0:T(8,128)(2,1)}, bf16[336,4096]{1,0:T(8,128)(2,1)}) custom-call(bf16[768,4096]{1,0:T(8,128)(2,1)} %copy-done.7, bf16[768,4096]{1,0:T(8,128)(2,1)} %copy-done.8, bf16[256,4096]{1,0:T(8,128)(2,1)S(1)} %copy-done.6, bf16[256,4096]{1,0:T(8,128)(2,1)S(1)} %copy-done.10, ...), custom_call_target="tpu_custom_call" | custom-call | flops 68719476736 | bytes 65536 | tf_op jit(solution)/shard_map/pallas_call | solution.py:211
  171.9 2.4 %collective-permute-start.26 = (bf16[64,4096]{1,0:T(8,128)(2,1)S(1)}, bf16[64,4096]{1,0:T(8,128)(2,1)S(1)}, u32[]{:S(2)}, u32[]{:S(2)}) collective-permute-start(bf16[64,4096]{1,0:T(8,128)(2,1)S(1)} %add_convert_fusion.2), channel_id=1, source_target_pairs={{16,0},{32,16},{48,32},{17,1},{33,17},{49,33},{18,2},{34,18},{50,3... | collective-permute-start | bytes 1572872 | tf_op jit(solution)/shard_map/ppermute | solution.py:327
  174.3 2.2 %copy-done.12 = bf16[512,4096]{1,0:T(8,128)(2,1)S(1)} copy-done((bf16[512,4096]{1,0:T(8,128)(2,1)S(1)}, bf16[512,4096]{1,0:T(8,128)(2,1)}, u32[]{:S(2)}) %copy-start.12) | copy-done | bytes 4194328
  176.5 12.7 %shard_map.110 = (bf16[336,4096]{1,0:T(8,128)(2,1)}, bf16[336,4096]{1,0:T(8,128)(2,1)}, bf16[336,4096]{1,0:T(8,128)(2,1)}) custom-call(bf16[768,4096]{1,0:T(8,128)(2,1)} %copy-done.7, bf16[768,4096]{1,0:T(8,128)(2,1)} %copy-done.8, bf16[256,4096]{1,0:T(8,128)(2,1)S(1)} %copy-done.6, ...), custom_call_target="tpu_custom_call", output_to_operand_aliasing={{0}: (20, {}), {1}: (21, {}), {2}: (22, {})} | custom-call | flops 68719476736 | bytes 65536 | tf_op jit(solution)/shard_map/pallas_call | solution.py:211
  189.2 2.1 %fusion = bf16[1,1,256,4096]{3,2,1,0:T(8,128)(2,1)} fusion(bf16[64,4096]{1,0:T(8,128)(2,1)S(1)} %collective-permute-done.26, s32[64]{0:T(128)S(1)} %copy-done.28, s32[256]{0:T(256)S(1)} %copy-done.30), kind=kOutput, calls=%fused_computation.2 | convolution fusion | flops 135282688 | bytes 2622720 | tf_op jit(solution)/shard_map/dot_general | solution.py:58
  (122 shorter events, 3.2 us)
Async XLA Ops:
  0.6 1.6 copy-start
  0.7 17.1 %copy-start.27 = (s32[64]{0:T(128)}, s32[64]{0:T(128)S(1)}, u32[]{:S(2)}) copy-start(s32[64]{0:T(128)S(1)} %iota_add_fusion) | copy-start | bytes 772
  1.6 1.7 copy-start.18
  3.9 13.7 %collective-permute-start = (bf16[64,4096]{1,0:T(8,128)(2,1)S(1)}, bf16[64,4096]{1,0:T(8,128)(2,1)S(1)}, u32[]{:S(2)}, u32[]{:S(2)}) collective-permute-start(bf16[64,4096]{1,0:T(8,128)(2,1)S(1)} %convolution_convert_fusion.2), channel_id=1, source_target_pairs={{0,66},{1,67},{4,70},{5,71},{8,74},{9,75},{12,78},{13,79},{2,64},{... | collective-permute-start | bytes 1572872 | tf_op jit(solution)/shard_map/ppermute | solution.py:38
  4.6 13.4 %collective-permute-start.3 = (bf16[64,4096]{1,0:T(8,128)(2,1)S(1)}, bf16[64,4096]{1,0:T(8,128)(2,1)S(1)}, u32[]{:S(2)}, u32[]{:S(2)}) collective-permute-start(bf16[64,4096]{1,0:T(8,128)(2,1)S(1)} %convolution_convert_fusion.2), channel_id=1, source_target_pairs={{0,2},{1,3},{4,6},{5,7},{8,10},{9,11},{12,14},{13,15},{2,0},{3,1},... | collective-permute-start | bytes 1572872 | tf_op jit(solution)/shard_map/ppermute | solution.py:38
  5.7 15.4 %collective-permute-start.1 = (bf16[64,4096]{1,0:T(8,128)(2,1)S(1)}, bf16[64,4096]{1,0:T(8,128)(2,1)S(1)}, u32[]{:S(2)}, u32[]{:S(2)}) collective-permute-start(bf16[64,4096]{1,0:T(8,128)(2,1)S(1)} %convolution_convert_fusion.1), channel_id=1, source_target_pairs={{0,4},{1,5},{4,8},{5,9},{8,12},{9,13},{12,0},{13,1},{2,6},{3,7},{6... | collective-permute-start | bytes 1572872 | tf_op jit(solution)/shard_map/ppermute | solution.py:38
  7.6 13.5 %collective-permute-start.2 = (bf16[64,4096]{1,0:T(8,128)(2,1)S(1)}, bf16[64,4096]{1,0:T(8,128)(2,1)S(1)}, u32[]{:S(2)}, u32[]{:S(2)}) collective-permute-start(bf16[64,4096]{1,0:T(8,128)(2,1)S(1)} %convolution_convert_fusion.1), channel_id=1, source_target_pairs={{0,12},{1,13},{4,0},{5,1},{8,4},{9,5},{12,8},{13,9},{2,14},{3,15},... | collective-permute-start | bytes 1572872 | tf_op jit(solution)/shard_map/ppermute | solution.py:38
  22.2 41.8 %collective-permute-start.4 = (bf16[224,4096]{1,0:T(8,128)(2,1)S(1)}, bf16[224,4096]{1,0:T(8,128)(2,1)S(1)}, u32[]{:S(2)}, u32[]{:S(2)}) collective-permute-start(bf16[224,4096]{1,0:T(8,128)(2,1)S(1)} %get-tuple-element.77), channel_id=1, source_target_pairs={{0,4},{1,5},{4,8},{5,9},{8,12},{9,13},{12,0},{13,1},{2,6},{3,7},{6... | collective-permute-start | bytes 5505032 | tf_op jit(solution)/shard_map/ppermute | solution.py:38
  23.5 40.6 %collective-permute-start.5 = (bf16[224,4096]{1,0:T(8,128)(2,1)S(1)}, bf16[224,4096]{1,0:T(8,128)(2,1)S(1)}, u32[]{:S(2)}, u32[]{:S(2)}) collective-permute-start(bf16[224,4096]{1,0:T(8,128)(2,1)S(1)} %get-tuple-element.78), channel_id=1, source_target_pairs={{0,12},{1,13},{4,0},{5,1},{8,4},{9,5},{12,8},{13,9},{2,14},{3,15},... | collective-permute-start | bytes 5505032 | tf_op jit(solution)/shard_map/ppermute | solution.py:38
  25.5 40.8 %collective-permute-start.7 = (bf16[224,4096]{1,0:T(8,128)(2,1)S(1)}, bf16[224,4096]{1,0:T(8,128)(2,1)S(1)}, u32[]{:S(2)}, u32[]{:S(2)}) collective-permute-start(bf16[224,4096]{1,0:T(8,128)(2,1)S(1)} %get-tuple-element.80), channel_id=1, source_target_pairs={{0,2},{1,3},{4,6},{5,7},{8,10},{9,11},{12,14},{13,15},{2,0},{3,1},... | collective-permute-start | bytes 5505032 | tf_op jit(solution)/shard_map/ppermute | solution.py:38
  26.4 39.7 %collective-permute-start.6 = (bf16[224,4096]{1,0:T(8,128)(2,1)S(1)}, bf16[224,4096]{1,0:T(8,128)(2,1)S(1)}, u32[]{:S(2)}, u32[]{:S(2)}) collective-permute-start(bf16[224,4096]{1,0:T(8,128)(2,1)S(1)} %get-tuple-element.79), channel_id=1, source_target_pairs={{0,66},{1,67},{4,70},{5,71},{8,74},{9,75},{12,78},{13,79},{2,64},{... | collective-permute-start | bytes 5505032 | tf_op jit(solution)/shard_map/ppermute | solution.py:38
  28.0 40.4 %collective-permute-start.8 = (s32[256]{0:T(256)S(1)}, s32[256]{0:T(256)S(1)}, u32[]{:S(2)}, u32[]{:S(2)}) collective-permute-start(s32[256]{0:T(256)S(1)} %broadcast_select_fusion), channel_id=1, source_target_pairs={{16,0},{32,16},{48,32},{17,1},{33,17},{49,33},{18,2},{34,18},{50,3... | collective-permute-start | bytes 3080 | tf_op jit(solution)/shard_map/ppermute | solution.py:266
  66.9 11.6 %copy-start.4 = (bf16[1,336,4096]{2,1,0:T(8,128)(2,1)S(1)}, bf16[1,336,4096]{2,1,0:T(8,128)(2,1)}, u32[]{:S(2)}) copy-start(bf16[1,336,4096]{2,1,0:T(8,128)(2,1)} %param.13) | copy-start | bytes 8257540
  67.3 11.2 %copy-start.3 = (bf16[1,336,4096]{2,1,0:T(8,128)(2,1)S(1)}, bf16[1,336,4096]{2,1,0:T(8,128)(2,1)}, u32[]{:S(2)}) copy-start(bf16[1,336,4096]{2,1,0:T(8,128)(2,1)} %param.12) | copy-start | bytes 8257540
  67.3 11.2 %copy-start.2 = (bf16[1,336,4096]{2,1,0:T(8,128)(2,1)S(1)}, bf16[1,336,4096]{2,1,0:T(8,128)(2,1)}, u32[]{:S(2)}) copy-start(bf16[1,336,4096]{2,1,0:T(8,128)(2,1)} %param.11) | copy-start | bytes 8257540
  67.5 19.1 %copy-start.7 = (bf16[768,4096]{1,0:T(8,128)(2,1)}, bf16[768,4096]{1,0:T(8,128)(2,1)S(1)}, u32[]{:S(2)}) copy-start(bf16[768,4096]{1,0:T(8,128)(2,1)S(1)} %slice_dynamic-update-slice_fusion.3.pair_ref.refs_0_) | copy-start | bytes 18874372
  68.4 18.3 %copy-start.29 = (s32[256]{0:T(256)}, s32[256]{0:T(256)S(1)}, u32[]{:S(2)}) copy-start(s32[256]{0:T(256)S(1)} %collective-permute-done.8) | copy-start | bytes 3076
  68.4 10.2 %collective-permute-start.9 = (bf16[768,4096]{1,0:T(8,128)(2,1)S(1)}, bf16[768,4096]{1,0:T(8,128)(2,1)S(1)}, u32[]{:S(2)}, u32[]{:S(2)}) collective-permute-start(bf16[768,4096]{1,0:T(8,128)(2,1)S(1)} %slice_dynamic-update-slice_fusion.3.pair_ref.refs_0_), channel_id=1, source_target_pairs={{0,1},{1,0},{4,5},{5,4},{8,9},{9,8},{12,13},{13,12},{2,3},{3,2},{6... | collective-permute-start | bytes 18874376 | tf_op jit(solution)/shard_map/ppermute | solution.py:38
  68.4 31.8 %collective-permute-start.10 = (bf16[160,4096]{1,0:T(8,128)(2,1)S(1)}, bf16[160,4096]{1,0:T(8,128)(2,1)S(1)}, u32[]{:S(2)}, u32[]{:S(2)}) collective-permute-start(bf16[160,4096]{1,0:T(8,128)(2,1)S(1)} %get-tuple-element.88), channel_id=1, source_target_pairs={{0,2},{1,3},{4,6},{5,7},{8,10},{9,11},{12,14},{13,15},{2,0},{3,1},... | collective-permute-start | bytes 3932168 | tf_op jit(solution)/shard_map/ppermute | solution.py:38
  70.8 31.2 %collective-permute-start.11 = (bf16[160,4096]{1,0:T(8,128)(2,1)S(1)}, bf16[160,4096]{1,0:T(8,128)(2,1)S(1)}, u32[]{:S(2)}, u32[]{:S(2)}) collective-permute-start(bf16[160,4096]{1,0:T(8,128)(2,1)S(1)} %get-tuple-element.89), channel_id=1, source_target_pairs={{0,66},{1,67},{4,70},{5,71},{8,74},{9,75},{12,78},{13,79},{2,64},{... | collective-permute-start | bytes 3932168 | tf_op jit(solution)/shard_map/ppermute | solution.py:38
  72.9 31.8 %collective-permute-start.12 = (bf16[160,4096]{1,0:T(8,128)(2,1)S(1)}, bf16[160,4096]{1,0:T(8,128)(2,1)S(1)}, u32[]{:S(2)}, u32[]{:S(2)}) collective-permute-start(bf16[160,4096]{1,0:T(8,128)(2,1)S(1)} %get-tuple-element.90), channel_id=1, source_target_pairs={{0,4},{1,5},{4,8},{5,9},{8,12},{9,13},{12,0},{13,1},{2,6},{3,7},{6... | collective-permute-start | bytes 3932168 | tf_op jit(solution)/shard_map/ppermute | solution.py:38
  73.0 31.8 %collective-permute-start.13 = (bf16[160,4096]{1,0:T(8,128)(2,1)S(1)}, bf16[160,4096]{1,0:T(8,128)(2,1)S(1)}, u32[]{:S(2)}, u32[]{:S(2)}) collective-permute-start(bf16[160,4096]{1,0:T(8,128)(2,1)S(1)} %get-tuple-element.91), channel_id=1, source_target_pairs={{0,12},{1,13},{4,0},{5,1},{8,4},{9,5},{12,8},{13,9},{2,14},{3,15},... | collective-permute-start | bytes 3932168 | tf_op jit(solution)/shard_map/ppermute | solution.py:38
  78.5 8.1 %copy-start.8 = (bf16[768,4096]{1,0:T(8,128)(2,1)}, bf16[768,4096]{1,0:T(8,128)(2,1)S(1)}, u32[]{:S(2)}) copy-start(bf16[768,4096]{1,0:T(8,128)(2,1)S(1)} %collective-permute-done.9.other_ref.refs_1_) | copy-start | bytes 18874372
  102.0 4.4 %copy-start.20 = (bf16[160,4096]{1,0:T(8,128)(2,1)}, bf16[160,4096]{1,0:T(8,128)(2,1)S(1)}, u32[]{:S(2)}) copy-start(bf16[160,4096]{1,0:T(8,128)(2,1)S(1)} %collective-permute-done.11) | copy-start | bytes 3932164
  104.7 1.1 copy-start.22
  104.7 1.5 copy-start.24
  106.4 4.3 %copy-start.5 = (bf16[256,4096]{1,0:T(8,128)(2,1)}, bf16[256,4096]{1,0:T(8,128)(2,1)S(1)}, u32[]{:S(2)}) copy-start(bf16[256,4096]{1,0:T(8,128)(2,1)S(1)} %pad_maximum_fusion.13.pair_ref.refs_2_) | copy-start | bytes 6291460
  106.4 4.2 %collective-permute-start.14 = (bf16[256,4096]{1,0:T(8,128)(2,1)S(1)}, bf16[256,4096]{1,0:T(8,128)(2,1)S(1)}, u32[]{:S(2)}, u32[]{:S(2)}) collective-permute-start(bf16[256,4096]{1,0:T(8,128)(2,1)S(1)} %pad_maximum_fusion.13.pair_ref.refs_2_), channel_id=1, source_target_pairs={{0,1},{1,0},{4,5},{5,4},{8,9},{9,8},{12,13},{13,12},{2,3},{3,2},{6... | collective-permute-start | bytes 6291464 | tf_op jit(solution)/shard_map/ppermute | solution.py:38
  107.0 10.2 %collective-permute-start.15 = (bf16[384,4096]{1,0:T(8,128)(2,1)S(1)}, bf16[384,4096]{1,0:T(8,128)(2,1)S(1)}, u32[]{:S(2)}, u32[]{:S(2)}) collective-permute-start(bf16[384,4096]{1,0:T(8,128)(2,1)S(1)} %get-tuple-element.99), channel_id=1, source_target_pairs={{0,1},{1,0},{4,5},{5,4},{8,9},{9,8},{12,13},{13,12},{2,3},{3,2},{6... | collective-permute-start | bytes 9437192 | tf_op jit(solution)/shard_map/ppermute | solution.py:38
  110.7 3.3 %copy-start.9 = (bf16[256,4096]{1,0:T(8,128)(2,1)}, bf16[256,4096]{1,0:T(8,128)(2,1)S(1)}, u32[]{:S(2)}) copy-start(bf16[256,4096]{1,0:T(8,128)(2,1)S(1)} %collective-permute-done.14.other_ref.refs_3_) | copy-start | bytes 6291460
  114.0 3.2 %copy-start.15 = (bf16[768,256]{1,0:T(8,128)(2,1)}, bf16[768,256]{1,0:T(8,128)(2,1)S(1)}, u32[]{:S(2)}) copy-start(bf16[768,256]{1,0:T(8,128)(2,1)S(1)} %get-tuple-element.97.grads_ref.refs_16_) | copy-start | bytes 1179652
  117.2 2.7 %collective-permute-start.16 = (bf16[128,4096]{1,0:T(8,128)(2,1)S(1)}, bf16[128,4096]{1,0:T(8,128)(2,1)S(1)}, u32[]{:S(2)}, u32[]{:S(2)}) collective-permute-start(bf16[128,4096]{1,0:T(8,128)(2,1)S(1)} %get-tuple-element.102), channel_id=1, source_target_pairs={{0,1},{1,0},{4,5},{5,4},{8,9},{9,8},{12,13},{13,12},{2,3},{3,2},{6... | collective-permute-start | bytes 3145736 | tf_op jit(solution)/shard_map/ppermute | solution.py:38
  119.9 1.3 copy-start.23
  119.9 1.7 copy-start.25
  120.2 1.9 %copy-start.19 = (bf16[64,4096]{1,0:T(8,128)(2,1)S(1)}, bf16[64,4096]{1,0:T(8,128)(2,1)}, u32[]{:S(2)}) copy-start(bf16[64,4096]{1,0:T(8,128)(2,1)} %pad_maximum_fusion.22) | copy-start | bytes 1572868
  120.2 2.0 %copy-start.21 = (bf16[160,4096]{1,0:T(8,128)(2,1)S(1)}, bf16[160,4096]{1,0:T(8,128)(2,1)}, u32[]{:S(2)}) copy-start(bf16[160,4096]{1,0:T(8,128)(2,1)} %copy-done.20) | copy-start | bytes 3932164
  121.7 5.8 %copy-start.26 = (bf16[128,4096]{1,0:T(8,128)(2,1)S(1)}, bf16[128,4096]{1,0:T(8,128)(2,1)}, u32[]{:S(2)}) copy-start(bf16[128,4096]{1,0:T(8,128)(2,1)} %pad_maximum_fusion.21) | copy-start | bytes 3145732
  121.7 5.7 %collective-permute-start.17 = (bf16[384,4096]{1,0:T(8,128)(2,1)S(1)}, bf16[384,4096]{1,0:T(8,128)(2,1)S(1)}, u32[]{:S(2)}, u32[]{:S(2)}) collective-permute-start(bf16[384,4096]{1,0:T(8,128)(2,1)S(1)} %pad_maximum_fusion.pair_ref.refs_4_), channel_id=1, source_target_pairs={{0,1},{1,0},{4,5},{5,4},{8,9},{9,8},{12,13},{13,12},{2,3},{3,2},{6... | collective-permute-start | bytes 9437192 | tf_op jit(solution)/shard_map/ppermute | solution.py:38
  122.4 11.0 %collective-permute-start.18 = (bf16[512,4096]{1,0:T(8,128)(2,1)S(1)}, bf16[512,4096]{1,0:T(8,128)(2,1)S(1)}, u32[]{:S(2)}, u32[]{:S(2)}) collective-permute-start(bf16[512,4096]{1,0:T(8,128)(2,1)S(1)} %slice_dynamic-update-slice_fusion.6.pair_ref.refs_6_), channel_id=1, source_target_pairs={{0,1},{1,0},{4,5},{5,4},{8,9},{9,8},{12,13},{13,12},{2,3},{3,2},{6... | collective-permute-start | bytes 12582920 | tf_op jit(solution)/shard_map/ppermute | solution.py:38
  122.8 25.6 %collective-permute-start.19 = (bf16[128,4096]{1,0:T(8,128)(2,1)}, bf16[128,4096]{1,0:T(8,128)(2,1)S(1)}, u32[]{:S(2)}, u32[]{:S(2)}) collective-permute-start(bf16[128,4096]{1,0:T(8,128)(2,1)} %get-tuple-element.111), channel_id=1, source_target_pairs={{0,12},{1,13},{4,0},{5,1},{8,4},{9,5},{12,8},{13,9},{2,14},{3,15},... | collective-permute-start | bytes 3145736 | tf_op jit(solution)/shard_map/ppermute | solution.py:38
  125.3 26.1 %collective-permute-start.20 = (bf16[128,4096]{1,0:T(8,128)(2,1)S(1)}, bf16[128,4096]{1,0:T(8,128)(2,1)S(1)}, u32[]{:S(2)}, u32[]{:S(2)}) collective-permute-start(bf16[128,4096]{1,0:T(8,128)(2,1)S(1)} %get-tuple-element.112), channel_id=1, source_target_pairs={{0,4},{1,5},{4,8},{5,9},{8,12},{9,13},{12,0},{13,1},{2,6},{3,7},{6... | collective-permute-start | bytes 3145736 | tf_op jit(solution)/shard_map/ppermute | solution.py:38
  125.3 13.7 %collective-permute-start.21 = (bf16[64,4096]{1,0:T(8,128)(2,1)S(1)}, bf16[64,4096]{1,0:T(8,128)(2,1)S(1)}, u32[]{:S(2)}, u32[]{:S(2)}) collective-permute-start(bf16[64,4096]{1,0:T(8,128)(2,1)S(1)} %get-tuple-element.113), channel_id=1, source_target_pairs={{0,2},{1,3},{4,6},{5,7},{8,10},{9,11},{12,14},{13,15},{2,0},{3,1},... | collective-permute-start | bytes 1572872 | tf_op jit(solution)/shard_map/ppermute | solution.py:38
  127.4 5.8 %copy-start.13 = (bf16[384,4096]{1,0:T(8,128)(2,1)}, bf16[384,4096]{1,0:T(8,128)(2,1)S(1)}, u32[]{:S(2)}) copy-start(bf16[384,4096]{1,0:T(8,128)(2,1)S(1)} %collective-permute-done.17.other_ref.refs_5_) | copy-start | bytes 9437188
  127.4 25.4 %collective-permute-start.22 = (bf16[128,4096]{1,0:T(8,128)(2,1)S(1)}, bf16[128,4096]{1,0:T(8,128)(2,1)S(1)}, u32[]{:S(2)}, u32[]{:S(2)}) collective-permute-start(bf16[128,4096]{1,0:T(8,128)(2,1)S(1)} %copy-done.26), channel_id=1, source_target_pairs={{0,66},{1,67},{4,70},{5,71},{8,74},{9,75},{12,78},{13,79},{2,64},{... | collective-permute-start | bytes 3145736 | tf_op jit(solution)/shard_map/ppermute | solution.py:38
  133.4 25.6 %copy-start.11 = (bf16[512,4096]{1,0:T(8,128)(2,1)}, bf16[512,4096]{1,0:T(8,128)(2,1)S(1)}, u32[]{:S(2)}) copy-start(bf16[512,4096]{1,0:T(8,128)(2,1)S(1)} %collective-permute-done.18.other_ref.refs_7_) | copy-start | bytes 12582916
  151.9 7.1 %copy-start.17 = (f32[128,4096]{1,0:T(8,128)}, f32[128,4096]{1,0:T(8,128)S(1)}, u32[]{:S(2)}) copy-start(f32[128,4096]{1,0:T(8,128)S(1)} %convert_add_fusion) | copy-start | bytes 6291460
  152.1 6.9 %copy-start.6 = (bf16[256,4096]{1,0:T(8,128)(2,1)S(1)}, bf16[256,4096]{1,0:T(8,128)(2,1)}, u32[]{:S(2)}) copy-start(bf16[256,4096]{1,0:T(8,128)(2,1)} %copy-done.5) | copy-start | bytes 6291460
  152.1 6.9 %copy-start.10 = (bf16[256,4096]{1,0:T(8,128)(2,1)S(1)}, bf16[256,4096]{1,0:T(8,128)(2,1)}, u32[]{:S(2)}) copy-start(bf16[256,4096]{1,0:T(8,128)(2,1)} %copy-done.9) | copy-start | bytes 6291460
  152.1 6.9 %copy-start.14 = (bf16[384,4096]{1,0:T(8,128)(2,1)S(1)}, bf16[384,4096]{1,0:T(8,128)(2,1)}, u32[]{:S(2)}) copy-start(bf16[384,4096]{1,0:T(8,128)(2,1)} %copy-done.13) | copy-start | bytes 9437188
  152.1 6.9 %copy-start.16 = (bf16[768,256]{1,0:T(8,128)(2,1)S(1)}, bf16[768,256]{1,0:T(8,128)(2,1)}, u32[]{:S(2)}) copy-start(bf16[768,256]{1,0:T(8,128)(2,1)} %copy-done.15) | copy-start | bytes 1179652
  152.8 3.1 %collective-permute-start.23 = (bf16[128,4096]{1,0:T(8,128)(2,1)S(1)}, bf16[128,4096]{1,0:T(8,128)(2,1)S(1)}, u32[]{:S(2)}, u32[]{:S(2)}) collective-permute-start(bf16[128,4096]{1,0:T(8,128)(2,1)S(1)} %collective-permute-done.22.pair_ref.refs_8_), channel_id=1, source_target_pairs={{0,1},{1,0},{4,5},{5,4},{8,9},{9,8},{12,13},{13,12},{2,3},{3,2},{6... | collective-permute-start | bytes 3145736 | tf_op jit(solution)/shard_map/ppermute | solution.py:38
  152.8 18.9 %collective-permute-start.24 = (bf16[64,4096]{1,0:T(8,128)(2,1)S(1)}, bf16[64,4096]{1,0:T(8,128)(2,1)S(1)}, u32[]{:S(2)}, u32[]{:S(2)}) collective-permute-start(bf16[64,4096]{1,0:T(8,128)(2,1)S(1)} %slice.206), channel_id=1, source_target_pairs={{0,2},{1,3},{4,6},{5,7},{8,10},{9,11},{12,14},{13,15},{2,0},{3,1},... | collective-permute-start | bytes 1572872 | tf_op jit(solution)/shard_map/ppermute | solution.py:38
  154.9 16.8 %collective-permute-start.25 = (bf16[64,4096]{1,0:T(8,128)(2,1)S(1)}, bf16[64,4096]{1,0:T(8,128)(2,1)S(1)}, u32[]{:S(2)}, u32[]{:S(2)}) collective-permute-start(bf16[64,4096]{1,0:T(8,128)(2,1)S(1)} %add_convert_fusion.3), channel_id=1, source_target_pairs={{0,8},{1,9},{4,12},{5,13},{8,0},{9,1},{12,4},{13,5},{2,10},{3,11},... | collective-permute-start | bytes 1572872 | tf_op jit(solution)/shard_map/ppermute | solution.py:38
  159.0 12.7 %slice-start = ((f32[128,4096]{1,0:T(8,128)}), f32[64,4096]{1,0:T(8,128)S(1)}, s32[]{:S(2)}) async-start(f32[128,4096]{1,0:T(8,128)} %copy-done.17), calls=%async_computation | async-start | bytes 2097152 | tf_op jit(solution)/shard_map/slice | solution.py:313
  171.9 17.3 %collective-permute-start.26 = (bf16[64,4096]{1,0:T(8,128)(2,1)S(1)}, bf16[64,4096]{1,0:T(8,128)(2,1)S(1)}, u32[]{:S(2)}, u32[]{:S(2)}) collective-permute-start(bf16[64,4096]{1,0:T(8,128)(2,1)S(1)} %add_convert_fusion.2), channel_id=1, source_target_pairs={{16,0},{32,16},{48,32},{17,1},{33,17},{49,33},{18,2},{34,18},{50,3... | collective-permute-start | bytes 1572872 | tf_op jit(solution)/shard_map/ppermute | solution.py:327
  174.3 2.2 %copy-start.12 = (bf16[512,4096]{1,0:T(8,128)(2,1)S(1)}, bf16[512,4096]{1,0:T(8,128)(2,1)}, u32[]{:S(2)}) copy-start(bf16[512,4096]{1,0:T(8,128)(2,1)} %copy-done.11) | copy-start | bytes 12582916
  176.5 12.7 %copy-start.28 = (s32[64]{0:T(128)S(1)}, s32[64]{0:T(128)}, u32[]{:S(2)}) copy-start(s32[64]{0:T(128)} %copy-done.27) | copy-start | bytes 772
  176.5 12.7 %copy-start.30 = (s32[256]{0:T(256)S(1)}, s32[256]{0:T(256)}, u32[]{:S(2)}) copy-start(s32[256]{0:T(256)} %copy-done.29) | copy-start | bytes 3076
  176.5 14.8 %copy-start.1 = (bf16[1,1,256,4096]{3,2,1,0:T(8,128)(2,1)S(1)}, bf16[1,1,256,4096]{3,2,1,0:T(8,128)(2,1)}, u32[]{:S(2)}) copy-start(bf16[1,1,256,4096]{3,2,1,0:T(8,128)(2,1)} %param.7) | copy-start | bytes 6291460

commit v2 on v1

--- a/solution.py
+++ b/solution.py
@@ -67,7 +67,7 @@
 
 
 GAP = 384
-FWD, TERM, SUMS = 14, 10, 24
+FWD, TERM, SUMS = 14, 10, 44
 ON_CHIP = pl.BlockSpec(memory_space=pltpu.VMEM)
 
 
@@ -204,9 +204,7 @@
         up_out[...] = both[units:]
         down_out[...] = half(matmul(hidden[...], rows_grads[slot]))
 
-    whole = [
-        pl.BlockSpec(v.shape, lambda j: (0, 0), pipeline_mode=pl.Buffered(1)) for v in hiddens + grads
-    ]
+    whole = [ON_CHIP] * len(hiddens + grads)
     hbm = pl.BlockSpec(memory_space=pl.ANY)
     return pl.pallas_call(
         kernel,
@@ -280,47 +278,44 @@
     more_i, more_o, more_b, more_u = send(to_i, INNER), send(to_o, OUTER), send(to_u, UP), send(to_b, DOWN)
     own_other = send(own_pair, SIBLING)
     hidden_own, grads_own = forward(own_pair, own_other, *weights, 1 << 20)
-    term_own, term_own2 = input_terms(grads_own, gate_local, up_local, 1 << 36)
+    term_own, term_own2 = input_terms(grads_own, gate_local, up_local, 1 << 20)
     term_own, term_own2, more_i, more_o, more_b, more_u = together(
         term_own, term_own2, more_i, more_o, more_b, more_u
     )
+    a_tt, g_tt = send(more_u[:64], OUTER), send(more_o[:64], INNER)
     far_pair = join(more_b[:64], more_u[:64], g_st, more_i[:64])
-    to_o = join(more_u[:64], more_i[:64])
     far_other = send(far_pair, SIBLING)
     term_from = send(term_own2, SIBLING)
-    hidden_far, grads_far = forward(far_pair, far_other, *weights, 1 << 20)
-    term_far, term_far2 = input_terms(grads_far, gate_local, up_local, 1 << 36)
+    hidden_far, grads_far = forward(far_pair, far_other, *weights, 1 << 36)
+    term_far, term_far2 = input_terms(grads_far, gate_local, up_local, 1 << 20)
     term_far2, term_from = together(term_far2, term_from)
     far_from = send(term_far2, SIBLING)
     own = half(full(term_own) + full(term_from))
     far = half(full(term_far) + full(far_from))
-    to_b, to_u, to_i, own0, far0, to_o, more_i, more_o, more_b, more_u, x1_pair = together(
-        own[128:256], own[256:384], far[64:128], own[:128], far[:64], to_o,
+    to_b, to_u, to_i, own0, far0, a_tt, g_tt, more_i, more_o, more_b, more_u, x1_pair = together(
+        own[128:256], own[256:384], far[64:128], own[:128], far[:64], a_tt, g_tt,
         more_i, more_o, more_b, more_u, x1_pair,
     )
-    z_u, z_b, far_i, tt = send(to_b, DOWN), send(to_u, UP), send(to_i, INNER), send(to_o, OUTER)
+    z_u, z_b, far_i = send(to_b, DOWN), send(to_u, UP), send(to_i, INNER)
     x1_other = send(x1_pair, SIBLING)
+    x1_other, more_b, more_u, a_tt = together(x1_other, more_b, more_u, a_tt)
     x2_pair = join(
-        more_b[64:160], more_u[128:160], more_u[64:128], a_ts,
-        more_i[128:160], more_o[64:96], more_o[:64], more_o[96:160], more_i[64:128],
+        more_b[64:160], more_u[128:160], more_u[64:128], a_ts, a_tt,
+        more_i[128:160], more_o[64:96], more_o[:64], more_o[96:160], more_i[64:128], g_tt,
     )
     x2_other = send(x2_pair, SIBLING)
     hidden_x1, grads_x1 = forward(x1_pair, x1_other, *weights, 1 << 36)
     hidden_x2, grads_x2 = forward(x2_pair, x2_other, *weights, 1 << 36)
     z_u, z_b, far_i, hidden_x1, hidden_x2 = together(z_u, z_b, far_i, hidden_x1, hidden_x2)
     near = full(own0) + full(z_u) + full(z_b)
-    to_i, to_t, near_s, x3_pair = together(
-        half(near[64:]), half(full(far0) + full(far_i)), near[:64], tt
-    )
-    x3_other = send(x3_pair, SIBLING)
-    hidden_x3, grads_x3 = forward(x3_pair, x3_other, *weights, 1 << 36)
+    to_i, to_t, near_s = together(half(near[64:]), half(full(far0) + full(far_i)), near[:64])
     near_i, far_t = send(to_i, INNER), send(to_t, ACROSS)
     pairs = [
         own_pair, own_other, far_pair, far_other,
-        x1_pair, x1_other, x2_pair, x2_other, x3_pair, x3_other,
+        x1_pair, x1_other, x2_pair, x2_other,
     ]
-    hiddens = [hidden_own, hidden_far, hidden_x1, hidden_x2, hidden_x3]
-    grads = [grads_own, grads_far, grads_x1, grads_x2, grads_x3]
+    hiddens = [hidden_own, hidden_far, hidden_x1, hidden_x2]
+    grads = [grads_own, grads_far, grads_x1, grads_x2]
     early = weight_grads(pairs, hiddens, grads, 0, 4, (), 1 << 36)
     near_i, far_t, near_s, early = together(near_i, far_t, near_s, tuple(early))
     input_rows = half(near_s + full(near_i) + full(far_t))

time: 192 us -> 189 us (0.984)
  local copies, waits for them, and re-layouts: 8.9 us -> 5.75 us
    unnamed x79 -> x93, local copies, waits for them, and re-layouts: 6.78 us -> 4.61 us
    concatenate x8 -> x7, other arithmetic: 4.12 us -> 3.13 us  [join(): return jnp.concatenate(parts, axis=0)]
    pallas_call x5 -> x4, Pallas kernels: 25.4 us -> 24.7 us  [forward(): pl.pallas_call(kernel, in_specs=[ON_CHIP] * 5, out_specs=[ON_CHIP] * 2, o...]
  transfers between devices with their start and end apart: 27 -> 27, of which waited for: 15 -> 18; matrix products, arithmetic and copies ran while one was open for 4% -> 3% of each run, Pallas kernels for 32% -> 32%
where the time goes in v2:
time: 189 us; the launch traced here: 187 us
  waiting for transfers between devices  76.2 us (40%)
  Pallas kernels  60 us (32%)
  starting transfers between devices  32.6 us (17%)
  other arithmetic  6.31 us (3%)
  local copies, waits for them, and re-layouts  5.75 us (3%)
  matrix products  4.81 us (3%)
    ppermute x25, waiting for transfers between devices, send(): return lax.ppermute(value, AXES, pairs)  76.2 us
    ppermute x25, starting transfers between devices, send(): return lax.ppermute(value, AXES, pairs)  27.8 us
    pallas_call x2, Pallas kernels, weight_grads(): pl.pallas_call(kernel, grid=(count,), in_specs=[hbm] * n + whole + [hbm]...  25.5 us
    pallas_call x4, Pallas kernels, forward(): pl.pallas_call(kernel, in_specs=[ON_CHIP] * 5, out_specs=[ON_CHIP] * 2, o...  24.7 us
    pallas_call x2, Pallas kernels, input_terms(): pl.pallas_call(kernel, in_specs=[ON_CHIP] * 3, out_specs=[ON_CHIP] * 2, o...  9.72 us
    dot_general x3, matrix products, matmul(): return jnp.dot(left, right, preferred_element_type=jnp.float32)  4.81 us
    unnamed x93, local copies, waits for them, and re-layouts  4.61 us
  transfers between devices with their start and end apart: 27, of which 18 were waited for; matrix products, arithmetic and copies ran while one was open for 3% of the time, Pallas kernels for 32%

profile of v2, /device:TPU:12, one launch (start us, length us, event | category | flops | bytes accessed | tf_op | source)
XLA Modules:
  0.0 187.1 jit_solution(1423351235831990773)
XLA Ops:
  0.7 0.9 select_reduce_fusion.1
  1.7 0.6 copy-done
  2.3 0.5 convolution_convert_fusion.2
  2.8 2.2 %convolution_convert_fusion.1 = bf16[64,4096]{1,0:T(8,128)(2,1)S(1)} fusion(bf16[1,1,256,4096]{3,2,1,0:T(8,128)(2,1)} %param.8, f32[256]{0:T(256)S(1)} %get-tuple-element.150, s32[256]{0:T(256)S(1)} %broadcast_select_fusion, s32[64]{0:T(128)S(1)} %iota_add_fusion), kind=kOutput, calls=%fused_computation.3 | convolution fusion | flops 137641984 | bytes 2623744 | tf_op jit(solution)/shard_map/dot_general | solution.py:58
  5.0 0.6 collective-permute-start
  5.6 1.1 collective-permute-start.3
  6.8 1.9 %collective-permute-start.1 = (bf16[64,4096]{1,0:T(8,128)(2,1)S(1)}, bf16[64,4096]{1,0:T(8,128)(2,1)S(1)}, u32[]{:S(2)}, u32[]{:S(2)}) collective-permute-start(bf16[64,4096]{1,0:T(8,128)(2,1)S(1)} %convolution_convert_fusion.1), channel_id=1, source_target_pairs={{0,4},{1,5},{4,8},{5,9},{8,12},{9,13},{12,0},{13,1},{2,6},{3,7},{6... | collective-permute-start | bytes 1572872 | tf_op jit(solution)/shard_map/ppermute | solution.py:38
  8.7 2.1 %collective-permute-start.2 = (bf16[64,4096]{1,0:T(8,128)(2,1)S(1)}, bf16[64,4096]{1,0:T(8,128)(2,1)S(1)}, u32[]{:S(2)}, u32[]{:S(2)}) collective-permute-start(bf16[64,4096]{1,0:T(8,128)(2,1)S(1)} %convolution_convert_fusion.1), channel_id=1, source_target_pairs={{0,12},{1,13},{4,0},{5,1},{8,4},{9,5},{12,8},{13,9},{2,14},{3,15},... | collective-permute-start | bytes 1572872 | tf_op jit(solution)/shard_map/ppermute | solution.py:38
  10.8 7.9 %collective-permute-done = bf16[64,4096]{1,0:T(8,128)(2,1)S(1)} collective-permute-done((bf16[64,4096]{1,0:T(8,128)(2,1)S(1)}, bf16[64,4096]{1,0:T(8,128)(2,1)S(1)}, u32[]{:S(2)}, u32[]{:S(2)}) %collective-permute-start) | collective-permute-done | bytes 524320 | tf_op jit(solution)/shard_map/ppermute | solution.py:38
  18.8 0.2 collective-permute-done.3
  19.0 3.1 %collective-permute-done.1 = bf16[64,4096]{1,0:T(8,128)(2,1)S(1)} collective-permute-done((bf16[64,4096]{1,0:T(8,128)(2,1)S(1)}, bf16[64,4096]{1,0:T(8,128)(2,1)S(1)}, u32[]{:S(2)}, u32[]{:S(2)}) %collective-permute-start.1) | collective-permute-done | bytes 524320 | tf_op jit(solution)/shard_map/ppermute | solution.py:38
  22.2 1.0 pad_maximum_fusion.1
  23.3 1.3 collective-permute-start.4
  24.6 2.0 %collective-permute-start.5 = (bf16[224,4096]{1,0:T(8,128)(2,1)S(1)}, bf16[224,4096]{1,0:T(8,128)(2,1)S(1)}, u32[]{:S(2)}, u32[]{:S(2)}) collective-permute-start(bf16[224,4096]{1,0:T(8,128)(2,1)S(1)} %get-tuple-element.80), channel_id=1, source_target_pairs={{0,12},{1,13},{4,0},{5,1},{8,4},{9,5},{12,8},{13,9},{2,14},{3,15},... | collective-permute-start | bytes 5505032 | tf_op jit(solution)/shard_map/ppermute | solution.py:38
  26.6 0.9 collective-permute-start.7
  27.5 1.5 collective-permute-start.6
  29.0 2.3 %collective-permute-start.8 = (s32[256]{0:T(256)S(1)}, s32[256]{0:T(256)S(1)}, u32[]{:S(2)}, u32[]{:S(2)}) collective-permute-start(s32[256]{0:T(256)S(1)} %broadcast_select_fusion), channel_id=1, source_target_pairs={{16,0},{32,16},{48,32},{17,1},{33,17},{49,33},{18,2},{34,18},{50,3... | collective-permute-start | bytes 3080 | tf_op jit(solution)/shard_map/ppermute | solution.py:264
  31.5 33.7 %collective-permute-done.4 = bf16[224,4096]{1,0:T(8,128)(2,1)S(1)} collective-permute-done((bf16[224,4096]{1,0:T(8,128)(2,1)S(1)}, bf16[224,4096]{1,0:T(8,128)(2,1)S(1)}, u32[]{:S(2)}, u32[]{:S(2)}) %collective-permute-start.4) | collective-permute-done | bytes 1835040 | tf_op jit(solution)/shard_map/ppermute | solution.py:38
  65.4 1.8 collective-permute-done.6
  67.5 0.3 pad_maximum_fusion.20
  68.0 0.4 fusion.7
  68.6 0.8 pad_maximum_fusion.21
  69.5 2.4 %collective-permute-start.10 = (bf16[160,4096]{1,0:T(8,128)(2,1)S(1)}, bf16[160,4096]{1,0:T(8,128)(2,1)S(1)}, u32[]{:S(2)}, u32[]{:S(2)}) collective-permute-start(bf16[160,4096]{1,0:T(8,128)(2,1)S(1)} %get-tuple-element.90), channel_id=1, source_target_pairs={{0,2},{1,3},{4,6},{5,7},{8,10},{9,11},{12,14},{13,15},{2,0},{3,1},... | collective-permute-start | bytes 3932168 | tf_op jit(solution)/shard_map/ppermute | solution.py:38
  71.9 2.1 %collective-permute-start.11 = (bf16[160,4096]{1,0:T(8,128)(2,1)S(1)}, bf16[160,4096]{1,0:T(8,128)(2,1)S(1)}, u32[]{:S(2)}, u32[]{:S(2)}) collective-permute-start(bf16[160,4096]{1,0:T(8,128)(2,1)S(1)} %get-tuple-element.91), channel_id=1, source_target_pairs={{0,66},{1,67},{4,70},{5,71},{8,74},{9,75},{12,78},{13,79},{2,64},{... | collective-permute-start | bytes 3932168 | tf_op jit(solution)/shard_map/ppermute | solution.py:38
  74.1 3.2 %collective-permute-start.13 = (bf16[160,4096]{1,0:T(8,128)(2,1)S(1)}, bf16[160,4096]{1,0:T(8,128)(2,1)S(1)}, u32[]{:S(2)}, u32[]{:S(2)}) collective-permute-start(bf16[160,4096]{1,0:T(8,128)(2,1)S(1)} %get-tuple-element.93), channel_id=1, source_target_pairs={{0,12},{1,13},{4,0},{5,1},{8,4},{9,5},{12,8},{13,9},{2,14},{3,15},... | collective-permute-start | bytes 3932168 | tf_op jit(solution)/shard_map/ppermute | solution.py:38
  77.3 2.3 %collective-permute-done.9.other_ref.refs_1_ = bf16[768,4096]{1,0:T(8,128)(2,1)S(1)} collective-permute-done((bf16[768,4096]{1,0:T(8,128)(2,1)S(1)}, bf16[768,4096]{1,0:T(8,128)(2,1)S(1)}, u32[]{:S(2)}, u32[]{:S(2)}) %collective-permute-start.9) | collective-permute-done | bytes 6291488 | tf_op jit(solution)/shard_map/ppermute | solution.py:38
  79.6 8.1 %shard_map.102 = (bf16[336,768]{1,0:T(8,128)(2,1)S(1)}, bf16[768,768]{1,0:T(8,128)(2,1)S(1)}) custom-call(bf16[768,4096]{1,0:T(8,128)(2,1)S(1)} %slice_dynamic-update-slice_fusion.3.pair_ref.refs_0_, bf16[768,4096]{1,0:T(8,128)(2,1)S(1)} %collective-permute-done.9.other_ref.refs_1_, bf16[336,4096]{1,0:T(8,128)(2,1)S(1)} %bitcast.18, ...), custom_call_target="tpu_custom_call" | custom-call | flops 1048576 | bytes 65536 | tf_op jit(solution)/shard_map/pallas_call | solution.py:106
  87.8 6.6 %shard_map.103 = (bf16[384,4096]{1,0:T(8,128)(2,1)S(1)}, bf16[384,4096]{1,0:T(8,128)(2,1)S(1)}) custom-call(bf16[768,768]{1,0:T(8,128)(2,1)S(1)} %get-tuple-element.87.grads_ref.refs_12_, bf16[336,4096]{1,0:T(8,128)(2,1)S(1)} %bitcast.19, bf16[336,4096]{1,0:T(8,128)(2,1)S(1)} %bitcast.25), custom_call_target="tpu_custom_call" | custom-call | flops 1048576 | bytes 65536 | tf_op jit(solution)/shard_map/pallas_call | solution.py:138
  94.4 6.9 %collective-permute-done.10 = bf16[160,4096]{1,0:T(8,128)(2,1)S(1)} collective-permute-done((bf16[160,4096]{1,0:T(8,128)(2,1)S(1)}, bf16[160,4096]{1,0:T(8,128)(2,1)S(1)}, u32[]{:S(2)}, u32[]{:S(2)}) %collective-permute-start.10) | collective-permute-done | bytes 1310752 | tf_op jit(solution)/shard_map/ppermute | solution.py:38
  101.3 1.9 %collective-permute-done.11 = bf16[160,4096]{1,0:T(8,128)(2,1)S(1)} collective-permute-done((bf16[160,4096]{1,0:T(8,128)(2,1)S(1)}, bf16[160,4096]{1,0:T(8,128)(2,1)S(1)}, u32[]{:S(2)}, u32[]{:S(2)}) %collective-permute-start.11) | collective-permute-done | bytes 1310752 | tf_op jit(solution)/shard_map/ppermute | solution.py:38
  103.2 2.7 %collective-permute-done.12 = bf16[160,4096]{1,0:T(8,128)(2,1)S(1)} collective-permute-done((bf16[160,4096]{1,0:T(8,128)(2,1)S(1)}, bf16[160,4096]{1,0:T(8,128)(2,1)S(1)}, u32[]{:S(2)}, u32[]{:S(2)}) %collective-permute-start.12) | collective-permute-done | bytes 1310752 | tf_op jit(solution)/shard_map/ppermute | solution.py:38
  105.9 1.0 copy-done.25
  107.1 0.2 copy-done.27
  107.4 0.4 pad_maximum_fusion.pair_ref.refs_4_
  107.8 0.4 collective-permute-start.17
  108.2 0.3 collective-permute-start.15
  108.6 1.4 collective-permute-start.18
  110.0 1.5 collective-permute-done.14.other_ref.refs_3_
  111.5 3.2 %shard_map.104 = (bf16[336,256]{1,0:T(8,128)(2,1)S(1)}, bf16[768,256]{1,0:T(8,128)(2,1)S(1)}) custom-call(bf16[256,4096]{1,0:T(8,128)(2,1)S(1)} %pad_maximum_fusion.13.pair_ref.refs_2_, bf16[256,4096]{1,0:T(8,128)(2,1)S(1)} %collective-permute-done.14.other_ref.refs_3_, bf16[336,4096]{1,0:T(8,128)(2,1)S(1)} %bitcast.20, bf16[336,4096]{1,0:T(8,128)(2,1)S(1)} %bitcast.26, ...), custom_call_target="tpu_custom_call" | custom-call | flops 68719476736 | bytes 65536 | tf_op jit(solution)/shard_map/pallas_call | solution.py:106
  114.7 3.2 %shard_map.105 = (bf16[128,4096]{1,0:T(8,128)(2,1)S(1)}, bf16[128,4096]{1,0:T(8,128)(2,1)S(1)}) custom-call(bf16[768,256]{1,0:T(8,128)(2,1)S(1)} %get-tuple-element.99.grads_ref.refs_13_, bf16[336,4096]{1,0:T(8,128)(2,1)S(1)} %bitcast.21, bf16[336,4096]{1,0:T(8,128)(2,1)S(1)} %bitcast.27), custom_call_target="tpu_custom_call" | custom-call | flops 1048576 | bytes 65536 | tf_op jit(solution)/shard_map/pallas_call | solution.py:138
  118.1 1.2 add_convert_fusion
  119.6 1.1 collective-permute-done.16
  120.7 0.2 add_convert_fusion.1
  121.0 1.2 collective-permute-done.17
  122.3 0.6 collective-permute-done.18
  122.8 0.2 copy-done.31
  123.1 0.6 copy-done.29
  123.7 2.5 %collective-permute-start.21 = (bf16[128,4096]{1,0:T(8,128)(2,1)S(1)}, bf16[128,4096]{1,0:T(8,128)(2,1)S(1)}, u32[]{:S(2)}, u32[]{:S(2)}) collective-permute-start(bf16[128,4096]{1,0:T(8,128)(2,1)S(1)} %get-tuple-element.120), channel_id=1, source_target_pairs={{0,12},{1,13},{4,0},{5,1},{8,4},{9,5},{12,8},{13,9},{2,14},{3,15},... | collective-permute-start | bytes 3145736 | tf_op jit(solution)/shard_map/ppermute | solution.py:38
  126.2 1.7 collective-permute-start.23
  127.9 1.4 collective-permute-done.19.other_ref.refs_5_
  129.8 1.1 copy-done.30
  131.0 0.2 collective-permute-start.20
  131.2 5.5 %shard_map.106 = (bf16[336,384]{1,0:T(8,128)(2,1)S(1)}, bf16[768,384]{1,0:T(8,128)(2,1)S(1)}) custom-call(bf16[384,4096]{1,0:T(8,128)(2,1)S(1)} %pad_maximum_fusion.pair_ref.refs_4_, bf16[384,4096]{1,0:T(8,128)(2,1)S(1)} %collective-permute-done.19.other_ref.refs_5_, bf16[336,4096]{1,0:T(8,128)(2,1)S(1)} %bitcast.22, bf16[336,4096]{1,0:T(8,128)(2,1)S(1)} %bitcast.28, ...), custom_call_target="tpu_custom_call" | custom-call | flops 68719476736 | bytes 65536 | tf_op jit(solution)/shard_map/pallas_call | solution.py:106
  136.7 3.0 %collective-permute-done.20.other_ref.refs_7_ = bf16[640,4096]{1,0:T(8,128)(2,1)S(1)} collective-permute-done((bf16[640,4096]{1,0:T(8,128)(2,1)S(1)}, bf16[640,4096]{1,0:T(8,128)(2,1)S(1)}, u32[]{:S(2)}, u32[]{:S(2)}) %collective-permute-start.20) | collective-permute-done | bytes 5242912 | tf_op jit(solution)/shard_map/ppermute | solution.py:38
  139.7 7.9 %shard_map.107 = (bf16[336,640]{1,0:T(8,128)(2,1)S(1)}, bf16[768,640]{1,0:T(8,128)(2,1)S(1)}) custom-call(bf16[640,4096]{1,0:T(8,128)(2,1)S(1)} %constant_dynamic-update-slice_fusion.5.pair_ref.refs_6_, bf16[640,4096]{1,0:T(8,128)(2,1)S(1)} %collective-permute-done.20.other_ref.refs_7_, bf16[336,4096]{1,0:T(8,128)(2,1)S(1)} %bitcast.23, ...), custom_call_target="tpu_custom_call" | custom-call | flops 68719476736 | bytes 65536 | tf_op jit(solution)/shard_map/pallas_call | solution.py:106
  147.7 1.6 collective-permute-done.21
  149.3 3.4 %collective-permute-done.22 = bf16[128,4096]{1,0:T(8,128)(2,1)S(1)} collective-permute-done((bf16[128,4096]{1,0:T(8,128)(2,1)S(1)}, bf16[128,4096]{1,0:T(8,128)(2,1)S(1)}, u32[]{:S(2)}, u32[]{:S(2)}) %collective-permute-start.22) | collective-permute-done | bytes 1048608 | tf_op jit(solution)/shard_map/ppermute | solution.py:38
  152.7 0.4 convert_add_fusion
  153.4 1.8 collective-permute-start.24
  155.2 12.8 %shard_map.108 = (bf16[336,4096]{1,0:T(8,128)(2,1)}, bf16[336,4096]{1,0:T(8,128)(2,1)}, bf16[336,4096]{1,0:T(8,128)(2,1)}) custom-call(bf16[768,4096]{1,0:T(8,128)(2,1)} %copy-done.4, bf16[768,4096]{1,0:T(8,128)(2,1)} %copy-done.5, bf16[256,4096]{1,0:T(8,128)(2,1)S(1)} %copy-done.9, bf16[256,4096]{1,0:T(8,128)(2,1)S(1)} %copy-done.18, ...), custom_call_target="tpu_custom_call" | custom-call | flops 68719476736 | bytes 65536 | tf_op jit(solution)/shard_map/pallas_call | solution.py:209
  168.0 1.6 collective-permute-done.25
  169.9 2.4 %collective-permute-start.26 = (bf16[64,4096]{1,0:T(8,128)(2,1)S(1)}, bf16[64,4096]{1,0:T(8,128)(2,1)S(1)}, u32[]{:S(2)}, u32[]{:S(2)}) collective-permute-start(bf16[64,4096]{1,0:T(8,128)(2,1)S(1)} %add_convert_fusion.2), channel_id=1, source_target_pairs={{16,0},{32,16},{48,32},{17,1},{33,17},{49,33},{18,2},{34,18},{50,3... | collective-permute-start | bytes 1572872 | tf_op jit(solution)/shard_map/ppermute | solution.py:322
  172.3 12.8 %shard_map.109 = (bf16[336,4096]{1,0:T(8,128)(2,1)}, bf16[336,4096]{1,0:T(8,128)(2,1)}, bf16[336,4096]{1,0:T(8,128)(2,1)}) custom-call(bf16[768,4096]{1,0:T(8,128)(2,1)} %copy-done.4, bf16[768,4096]{1,0:T(8,128)(2,1)} %copy-done.5, bf16[256,4096]{1,0:T(8,128)(2,1)S(1)} %copy-done.9, ...), custom_call_target="tpu_custom_call", output_to_operand_aliasing={{0}: (16, {}), {1}: (17, {}), {2}: (18, {})} | custom-call | flops 68719476736 | bytes 65536 | tf_op jit(solution)/shard_map/pallas_call | solution.py:209
  185.1 2.1 %fusion = bf16[1,1,256,4096]{3,2,1,0:T(8,128)(2,1)} fusion(bf16[64,4096]{1,0:T(8,128)(2,1)S(1)} %collective-permute-done.26, s32[64]{0:T(128)S(1)} %copy-done.34, s32[256]{0:T(256)S(1)} %copy-done.36), kind=kOutput, calls=%fused_computation.2 | convolution fusion | flops 135282688 | bytes 2622720 | tf_op jit(solution)/shard_map/dot_general | solution.py:58
  (134 shorter events, 2.9 us)
Async XLA Ops:
  0.6 1.6 copy-start
  0.7 18.4 %copy-start.33 = (s32[64]{0:T(128)}, s32[64]{0:T(128)S(1)}, u32[]{:S(2)}) copy-start(s32[64]{0:T(128)S(1)} %iota_add_fusion) | copy-start | bytes 772
  5.0 13.7 %collective-permute-start = (bf16[64,4096]{1,0:T(8,128)(2,1)S(1)}, bf16[64,4096]{1,0:T(8,128)(2,1)S(1)}, u32[]{:S(2)}, u32[]{:S(2)}) collective-permute-start(bf16[64,4096]{1,0:T(8,128)(2,1)S(1)} %convolution_convert_fusion.2), channel_id=1, source_target_pairs={{0,66},{1,67},{4,70},{5,71},{8,74},{9,75},{12,78},{13,79},{2,64},{... | collective-permute-start | bytes 1572872 | tf_op jit(solution)/shard_map/ppermute | solution.py:38
  5.6 13.4 %collective-permute-start.3 = (bf16[64,4096]{1,0:T(8,128)(2,1)S(1)}, bf16[64,4096]{1,0:T(8,128)(2,1)S(1)}, u32[]{:S(2)}, u32[]{:S(2)}) collective-permute-start(bf16[64,4096]{1,0:T(8,128)(2,1)S(1)} %convolution_convert_fusion.2), channel_id=1, source_target_pairs={{0,2},{1,3},{4,6},{5,7},{8,10},{9,11},{12,14},{13,15},{2,0},{3,1},... | collective-permute-start | bytes 1572872 | tf_op jit(solution)/shard_map/ppermute | solution.py:38
  6.8 15.4 %collective-permute-start.1 = (bf16[64,4096]{1,0:T(8,128)(2,1)S(1)}, bf16[64,4096]{1,0:T(8,128)(2,1)S(1)}, u32[]{:S(2)}, u32[]{:S(2)}) collective-permute-start(bf16[64,4096]{1,0:T(8,128)(2,1)S(1)} %convolution_convert_fusion.1), channel_id=1, source_target_pairs={{0,4},{1,5},{4,8},{5,9},{8,12},{9,13},{12,0},{13,1},{2,6},{3,7},{6... | collective-permute-start | bytes 1572872 | tf_op jit(solution)/shard_map/ppermute | solution.py:38
  8.7 13.5 %collective-permute-start.2 = (bf16[64,4096]{1,0:T(8,128)(2,1)S(1)}, bf16[64,4096]{1,0:T(8,128)(2,1)S(1)}, u32[]{:S(2)}, u32[]{:S(2)}) collective-permute-start(bf16[64,4096]{1,0:T(8,128)(2,1)S(1)} %convolution_convert_fusion.1), channel_id=1, source_target_pairs={{0,12},{1,13},{4,0},{5,1},{8,4},{9,5},{12,8},{13,9},{2,14},{3,15},... | collective-permute-start | bytes 1572872 | tf_op jit(solution)/shard_map/ppermute | solution.py:38
  23.3 41.8 %collective-permute-start.4 = (bf16[224,4096]{1,0:T(8,128)(2,1)S(1)}, bf16[224,4096]{1,0:T(8,128)(2,1)S(1)}, u32[]{:S(2)}, u32[]{:S(2)}) collective-permute-start(bf16[224,4096]{1,0:T(8,128)(2,1)S(1)} %get-tuple-element.79), channel_id=1, source_target_pairs={{0,4},{1,5},{4,8},{5,9},{8,12},{9,13},{12,0},{13,1},{2,6},{3,7},{6... | collective-permute-start | bytes 5505032 | tf_op jit(solution)/shard_map/ppermute | solution.py:38
  24.6 40.7 %collective-permute-start.5 = (bf16[224,4096]{1,0:T(8,128)(2,1)S(1)}, bf16[224,4096]{1,0:T(8,128)(2,1)S(1)}, u32[]{:S(2)}, u32[]{:S(2)}) collective-permute-start(bf16[224,4096]{1,0:T(8,128)(2,1)S(1)} %get-tuple-element.80), channel_id=1, source_target_pairs={{0,12},{1,13},{4,0},{5,1},{8,4},{9,5},{12,8},{13,9},{2,14},{3,15},... | collective-permute-start | bytes 5505032 | tf_op jit(solution)/shard_map/ppermute | solution.py:38
  26.6 40.8 %collective-permute-start.7 = (bf16[224,4096]{1,0:T(8,128)(2,1)S(1)}, bf16[224,4096]{1,0:T(8,128)(2,1)S(1)}, u32[]{:S(2)}, u32[]{:S(2)}) collective-permute-start(bf16[224,4096]{1,0:T(8,128)(2,1)S(1)} %get-tuple-element.82), channel_id=1, source_target_pairs={{0,2},{1,3},{4,6},{5,7},{8,10},{9,11},{12,14},{13,15},{2,0},{3,1},... | collective-permute-start | bytes 5505032 | tf_op jit(solution)/shard_map/ppermute | solution.py:38
  27.5 39.7 %collective-permute-start.6 = (bf16[224,4096]{1,0:T(8,128)(2,1)S(1)}, bf16[224,4096]{1,0:T(8,128)(2,1)S(1)}, u32[]{:S(2)}, u32[]{:S(2)}) collective-permute-start(bf16[224,4096]{1,0:T(8,128)(2,1)S(1)} %get-tuple-element.81), channel_id=1, source_target_pairs={{0,66},{1,67},{4,70},{5,71},{8,74},{9,75},{12,78},{13,79},{2,64},{... | collective-permute-start | bytes 5505032 | tf_op jit(solution)/shard_map/ppermute | solution.py:38
  29.0 40.4 %collective-permute-start.8 = (s32[256]{0:T(256)S(1)}, s32[256]{0:T(256)S(1)}, u32[]{:S(2)}, u32[]{:S(2)}) collective-permute-start(s32[256]{0:T(256)S(1)} %broadcast_select_fusion), channel_id=1, source_target_pairs={{16,0},{32,16},{48,32},{17,1},{33,17},{49,33},{18,2},{34,18},{50,3... | collective-permute-start | bytes 3080 | tf_op jit(solution)/shard_map/ppermute | solution.py:264
  68.0 11.7 %copy-start.7 = (bf16[1,336,4096]{2,1,0:T(8,128)(2,1)S(1)}, bf16[1,336,4096]{2,1,0:T(8,128)(2,1)}, u32[]{:S(2)}) copy-start(bf16[1,336,4096]{2,1,0:T(8,128)(2,1)} %param.13) | copy-start | bytes 8257540
  68.4 11.2 %copy-start.2 = (bf16[1,336,4096]{2,1,0:T(8,128)(2,1)S(1)}, bf16[1,336,4096]{2,1,0:T(8,128)(2,1)}, u32[]{:S(2)}) copy-start(bf16[1,336,4096]{2,1,0:T(8,128)(2,1)} %param.11) | copy-start | bytes 8257540
  68.4 11.2 %copy-start.3 = (bf16[1,336,4096]{2,1,0:T(8,128)(2,1)S(1)}, bf16[1,336,4096]{2,1,0:T(8,128)(2,1)}, u32[]{:S(2)}) copy-start(bf16[1,336,4096]{2,1,0:T(8,128)(2,1)} %param.12) | copy-start | bytes 8257540
  68.6 19.1 %copy-start.4 = (bf16[768,4096]{1,0:T(8,128)(2,1)}, bf16[768,4096]{1,0:T(8,128)(2,1)S(1)}, u32[]{:S(2)}) copy-start(bf16[768,4096]{1,0:T(8,128)(2,1)S(1)} %slice_dynamic-update-slice_fusion.3.pair_ref.refs_0_) | copy-start | bytes 18874372
  69.5 18.3 %copy-start.35 = (s32[256]{0:T(256)}, s32[256]{0:T(256)S(1)}, u32[]{:S(2)}) copy-start(s32[256]{0:T(256)S(1)} %collective-permute-done.8) | copy-start | bytes 3076
  69.5 10.2 %collective-permute-start.9 = (bf16[768,4096]{1,0:T(8,128)(2,1)S(1)}, bf16[768,4096]{1,0:T(8,128)(2,1)S(1)}, u32[]{:S(2)}, u32[]{:S(2)}) collective-permute-start(bf16[768,4096]{1,0:T(8,128)(2,1)S(1)} %slice_dynamic-update-slice_fusion.3.pair_ref.refs_0_), channel_id=1, source_target_pairs={{0,1},{1,0},{4,5},{5,4},{8,9},{9,8},{12,13},{13,12},{2,3},{3,2},{6... | collective-permute-start | bytes 18874376 | tf_op jit(solution)/shard_map/ppermute | solution.py:38
  69.5 31.8 %collective-permute-start.10 = (bf16[160,4096]{1,0:T(8,128)(2,1)S(1)}, bf16[160,4096]{1,0:T(8,128)(2,1)S(1)}, u32[]{:S(2)}, u32[]{:S(2)}) collective-permute-start(bf16[160,4096]{1,0:T(8,128)(2,1)S(1)} %get-tuple-element.90), channel_id=1, source_target_pairs={{0,2},{1,3},{4,6},{5,7},{8,10},{9,11},{12,14},{13,15},{2,0},{3,1},... | collective-permute-start | bytes 3932168 | tf_op jit(solution)/shard_map/ppermute | solution.py:38
  71.9 31.2 %collective-permute-start.11 = (bf16[160,4096]{1,0:T(8,128)(2,1)S(1)}, bf16[160,4096]{1,0:T(8,128)(2,1)S(1)}, u32[]{:S(2)}, u32[]{:S(2)}) collective-permute-start(bf16[160,4096]{1,0:T(8,128)(2,1)S(1)} %get-tuple-element.91), channel_id=1, source_target_pairs={{0,66},{1,67},{4,70},{5,71},{8,74},{9,75},{12,78},{13,79},{2,64},{... | collective-permute-start | bytes 3932168 | tf_op jit(solution)/shard_map/ppermute | solution.py:38
  74.0 31.8 %collective-permute-start.12 = (bf16[160,4096]{1,0:T(8,128)(2,1)S(1)}, bf16[160,4096]{1,0:T(8,128)(2,1)S(1)}, u32[]{:S(2)}, u32[]{:S(2)}) collective-permute-start(bf16[160,4096]{1,0:T(8,128)(2,1)S(1)} %get-tuple-element.92), channel_id=1, source_target_pairs={{0,4},{1,5},{4,8},{5,9},{8,12},{9,13},{12,0},{13,1},{2,6},{3,7},{6... | collective-permute-start | bytes 3932168 | tf_op jit(solution)/shard_map/ppermute | solution.py:38
  74.1 31.8 %collective-permute-start.13 = (bf16[160,4096]{1,0:T(8,128)(2,1)S(1)}, bf16[160,4096]{1,0:T(8,128)(2,1)S(1)}, u32[]{:S(2)}, u32[]{:S(2)}) collective-permute-start(bf16[160,4096]{1,0:T(8,128)(2,1)S(1)} %get-tuple-element.93), channel_id=1, source_target_pairs={{0,12},{1,13},{4,0},{5,1},{8,4},{9,5},{12,8},{13,9},{2,14},{3,15},... | collective-permute-start | bytes 3932168 | tf_op jit(solution)/shard_map/ppermute | solution.py:38
  79.6 8.1 %copy-start.5 = (bf16[768,4096]{1,0:T(8,128)(2,1)}, bf16[768,4096]{1,0:T(8,128)(2,1)S(1)}, u32[]{:S(2)}) copy-start(bf16[768,4096]{1,0:T(8,128)(2,1)S(1)} %collective-permute-done.9.other_ref.refs_1_) | copy-start | bytes 18874372
  87.8 6.6 %copy-start.10 = (bf16[768,768]{1,0:T(8,128)(2,1)}, bf16[768,768]{1,0:T(8,128)(2,1)S(1)}, u32[]{:S(2)}) copy-start(bf16[768,768]{1,0:T(8,128)(2,1)S(1)} %get-tuple-element.87.grads_ref.refs_12_) | copy-start | bytes 3538948
  101.3 5.8 %copy-start.23 = (bf16[160,4096]{1,0:T(8,128)(2,1)}, bf16[160,4096]{1,0:T(8,128)(2,1)S(1)}, u32[]{:S(2)}) copy-start(bf16[160,4096]{1,0:T(8,128)(2,1)S(1)} %collective-permute-done.10) | copy-start | bytes 3932164
  103.1 5.4 %copy-start.20 = (bf16[160,4096]{1,0:T(8,128)(2,1)}, bf16[160,4096]{1,0:T(8,128)(2,1)S(1)}, u32[]{:S(2)}) copy-start(bf16[160,4096]{1,0:T(8,128)(2,1)S(1)} %collective-permute-done.11) | copy-start | bytes 3932164
  105.8 1.1 copy-start.25
  105.8 1.5 copy-start.27
  107.3 4.2 %copy-start.8 = (bf16[256,4096]{1,0:T(8,128)(2,1)}, bf16[256,4096]{1,0:T(8,128)(2,1)S(1)}, u32[]{:S(2)}) copy-start(bf16[256,4096]{1,0:T(8,128)(2,1)S(1)} %pad_maximum_fusion.13.pair_ref.refs_2_) | copy-start | bytes 6291460
  107.3 4.2 %collective-permute-start.14 = (bf16[256,4096]{1,0:T(8,128)(2,1)S(1)}, bf16[256,4096]{1,0:T(8,128)(2,1)S(1)}, u32[]{:S(2)}, u32[]{:S(2)}) collective-permute-start(bf16[256,4096]{1,0:T(8,128)(2,1)S(1)} %pad_maximum_fusion.13.pair_ref.refs_2_), channel_id=1, source_target_pairs={{0,1},{1,0},{4,5},{5,4},{8,9},{9,8},{12,13},{13,12},{2,3},{3,2},{6... | collective-permute-start | bytes 6291464 | tf_op jit(solution)/shard_map/ppermute | solution.py:38
  107.8 23.4 %copy-start.6 = (bf16[384,4096]{1,0:T(8,128)(2,1)}, bf16[384,4096]{1,0:T(8,128)(2,1)S(1)}, u32[]{:S(2)}) copy-start(bf16[384,4096]{1,0:T(8,128)(2,1)S(1)} %pad_maximum_fusion.pair_ref.refs_4_) | copy-start | bytes 9437188
  107.8 14.4 %collective-permute-start.17 = (bf16[64,4096]{1,0:T(8,128)(2,1)S(1)}, bf16[64,4096]{1,0:T(8,128)(2,1)S(1)}, u32[]{:S(2)}, u32[]{:S(2)}) collective-permute-start(bf16[64,4096]{1,0:T(8,128)(2,1)S(1)} %slice.145), channel_id=1, source_target_pairs={{0,66},{1,67},{4,70},{5,71},{8,74},{9,75},{12,78},{13,79},{2,64},{... | collective-permute-start | bytes 1572872 | tf_op jit(solution)/shard_map/ppermute | solution.py:38
  108.2 9.7 %collective-permute-start.15 = (bf16[384,4096]{1,0:T(8,128)(2,1)S(1)}, bf16[384,4096]{1,0:T(8,128)(2,1)S(1)}, u32[]{:S(2)}, u32[]{:S(2)}) collective-permute-start(bf16[384,4096]{1,0:T(8,128)(2,1)S(1)} %get-tuple-element.101), channel_id=1, source_target_pairs={{0,1},{1,0},{4,5},{5,4},{8,9},{9,8},{12,13},{13,12},{2,3},{3,2},{6... | collective-permute-start | bytes 9437192 | tf_op jit(solution)/shard_map/ppermute | solution.py:38
  108.6 14.3 %collective-permute-start.18 = (bf16[64,4096]{1,0:T(8,128)(2,1)S(1)}, bf16[64,4096]{1,0:T(8,128)(2,1)S(1)}, u32[]{:S(2)}, u32[]{:S(2)}) collective-permute-start(bf16[64,4096]{1,0:T(8,128)(2,1)S(1)} %slice.152), channel_id=1, source_target_pairs={{0,2},{1,3},{4,6},{5,7},{8,10},{9,11},{12,14},{13,15},{2,0},{3,1},... | collective-permute-start | bytes 1572872 | tf_op jit(solution)/shard_map/ppermute | solution.py:38
  111.5 3.3 %copy-start.17 = (bf16[256,4096]{1,0:T(8,128)(2,1)}, bf16[256,4096]{1,0:T(8,128)(2,1)S(1)}, u32[]{:S(2)}) copy-start(bf16[256,4096]{1,0:T(8,128)(2,1)S(1)} %collective-permute-done.14.other_ref.refs_3_) | copy-start | bytes 6291460
  114.7 4.6 %copy-start.12 = (bf16[768,256]{1,0:T(8,128)(2,1)}, bf16[768,256]{1,0:T(8,128)(2,1)S(1)}, u32[]{:S(2)}) copy-start(bf16[768,256]{1,0:T(8,128)(2,1)S(1)} %get-tuple-element.99.grads_ref.refs_13_) | copy-start | bytes 1179652
  117.9 2.7 %collective-permute-start.16 = (bf16[128,4096]{1,0:T(8,128)(2,1)S(1)}, bf16[128,4096]{1,0:T(8,128)(2,1)S(1)}, u32[]{:S(2)}, u32[]{:S(2)}) collective-permute-start(bf16[128,4096]{1,0:T(8,128)(2,1)S(1)} %get-tuple-element.104), channel_id=1, source_target_pairs={{0,1},{1,0},{4,5},{5,4},{8,9},{9,8},{12,13},{13,12},{2,3},{3,2},{6... | collective-permute-start | bytes 3145736 | tf_op jit(solution)/shard_map/ppermute | solution.py:38
  119.6 9.8 %copy-start.26 = (bf16[160,4096]{1,0:T(8,128)(2,1)S(1)}, bf16[160,4096]{1,0:T(8,128)(2,1)}, u32[]{:S(2)}) copy-start(bf16[160,4096]{1,0:T(8,128)(2,1)} %copy-done.25) | copy-start | bytes 3932164
  120.7 8.7 %copy-start.28 = (bf16[160,4096]{1,0:T(8,128)(2,1)S(1)}, bf16[160,4096]{1,0:T(8,128)(2,1)}, u32[]{:S(2)}) copy-start(bf16[160,4096]{1,0:T(8,128)(2,1)} %copy-done.27) | copy-start | bytes 3932164
  120.9 8.5 %copy-start.22 = (bf16[64,4096]{1,0:T(8,128)(2,1)S(1)}, bf16[64,4096]{1,0:T(8,128)(2,1)}, u32[]{:S(2)}) copy-start(bf16[64,4096]{1,0:T(8,128)(2,1)} %pad_maximum_fusion.21) | copy-start | bytes 1572868
  121.0 8.6 %copy-start.24 = (bf16[160,4096]{1,0:T(8,128)(2,1)S(1)}, bf16[160,4096]{1,0:T(8,128)(2,1)}, u32[]{:S(2)}) copy-start(bf16[160,4096]{1,0:T(8,128)(2,1)} %copy-done.23) | copy-start | bytes 3932164
  121.0 8.6 %copy-start.21 = (bf16[160,4096]{1,0:T(8,128)(2,1)S(1)}, bf16[160,4096]{1,0:T(8,128)(2,1)}, u32[]{:S(2)}) copy-start(bf16[160,4096]{1,0:T(8,128)(2,1)} %copy-done.20) | copy-start | bytes 3932164
  122.3 0.8 copy-start.31
  122.8 0.8 copy-start.29
  123.7 5.9 %copy-start.32 = (bf16[64,4096]{1,0:T(8,128)(2,1)S(1)}, bf16[64,4096]{1,0:T(8,128)(2,1)}, u32[]{:S(2)}) copy-start(bf16[64,4096]{1,0:T(8,128)(2,1)} %copy-done.31) | copy-start | bytes 1572868
  123.7 5.7 %collective-permute-start.19 = (bf16[384,4096]{1,0:T(8,128)(2,1)S(1)}, bf16[384,4096]{1,0:T(8,128)(2,1)S(1)}, u32[]{:S(2)}, u32[]{:S(2)}) collective-permute-start(bf16[384,4096]{1,0:T(8,128)(2,1)S(1)} %pad_maximum_fusion.pair_ref.refs_4_), channel_id=1, source_target_pairs={{0,1},{1,0},{4,5},{5,4},{8,9},{9,8},{12,13},{13,12},{2,3},{3,2},{6... | collective-permute-start | bytes 9437192 | tf_op jit(solution)/shard_map/ppermute | solution.py:38
  123.7 25.6 %collective-permute-start.21 = (bf16[128,4096]{1,0:T(8,128)(2,1)S(1)}, bf16[128,4096]{1,0:T(8,128)(2,1)S(1)}, u32[]{:S(2)}, u32[]{:S(2)}) collective-permute-start(bf16[128,4096]{1,0:T(8,128)(2,1)S(1)} %get-tuple-element.120), channel_id=1, source_target_pairs={{0,12},{1,13},{4,0},{5,1},{8,4},{9,5},{12,8},{13,9},{2,14},{3,15},... | collective-permute-start | bytes 3145736 | tf_op jit(solution)/shard_map/ppermute | solution.py:38
  126.2 26.5 %collective-permute-start.22 = (bf16[128,4096]{1,0:T(8,128)(2,1)S(1)}, bf16[128,4096]{1,0:T(8,128)(2,1)S(1)}, u32[]{:S(2)}, u32[]{:S(2)}) collective-permute-start(bf16[128,4096]{1,0:T(8,128)(2,1)S(1)} %get-tuple-element.121), channel_id=1, source_target_pairs={{0,4},{1,5},{4,8},{5,9},{8,12},{9,13},{12,0},{13,1},{2,6},{3,7},{6... | collective-permute-start | bytes 3145736 | tf_op jit(solution)/shard_map/ppermute | solution.py:38
  126.2 21.5 %collective-permute-start.23 = (bf16[64,4096]{1,0:T(8,128)(2,1)S(1)}, bf16[64,4096]{1,0:T(8,128)(2,1)S(1)}, u32[]{:S(2)}, u32[]{:S(2)}) collective-permute-start(bf16[64,4096]{1,0:T(8,128)(2,1)S(1)} %get-tuple-element.122), channel_id=1, source_target_pairs={{0,2},{1,3},{4,6},{5,7},{8,10},{9,11},{12,14},{13,15},{2,0},{3,1},... | collective-permute-start | bytes 1572872 | tf_op jit(solution)/shard_map/ppermute | solution.py:38
  129.3 1.9 copy-start.16
  129.5 1.4 copy-start.30
  131.0 8.8 %copy-start.14 = (bf16[640,4096]{1,0:T(8,128)(2,1)}, bf16[640,4096]{1,0:T(8,128)(2,1)S(1)}, u32[]{:S(2)}) copy-start(bf16[640,4096]{1,0:T(8,128)(2,1)S(1)} %constant_dynamic-update-slice_fusion.5.pair_ref.refs_6_) | copy-start | bytes 15728644
  131.0 8.7 %collective-permute-start.20 = (bf16[640,4096]{1,0:T(8,128)(2,1)S(1)}, bf16[640,4096]{1,0:T(8,128)(2,1)S(1)}, u32[]{:S(2)}, u32[]{:S(2)}) collective-permute-start(bf16[640,4096]{1,0:T(8,128)(2,1)S(1)} %constant_dynamic-update-slice_fusion.5.pair_ref.refs_6_), channel_id=1, source_target_pairs={{0,1},{1,0},{4,5},{5,4},{8,9},{9,8},{12,13},{13,12},{2,3},{3,2},{6... | collective-permute-start | bytes 15728648 | tf_op jit(solution)/shard_map/ppermute | solution.py:38
  139.7 7.9 %copy-start.15 = (bf16[640,4096]{1,0:T(8,128)(2,1)}, bf16[640,4096]{1,0:T(8,128)(2,1)S(1)}, u32[]{:S(2)}) copy-start(bf16[640,4096]{1,0:T(8,128)(2,1)S(1)} %collective-permute-done.20.other_ref.refs_7_) | copy-start | bytes 15728644
  139.7 15.5 %copy-start.18 = (bf16[256,4096]{1,0:T(8,128)(2,1)S(1)}, bf16[256,4096]{1,0:T(8,128)(2,1)}, u32[]{:S(2)}) copy-start(bf16[256,4096]{1,0:T(8,128)(2,1)} %copy-done.17) | copy-start | bytes 6291460
  153.1 2.1 %copy-start.9 = (bf16[256,4096]{1,0:T(8,128)(2,1)S(1)}, bf16[256,4096]{1,0:T(8,128)(2,1)}, u32[]{:S(2)}) copy-start(bf16[256,4096]{1,0:T(8,128)(2,1)} %copy-done.8) | copy-start | bytes 6291460
  153.1 2.1 %copy-start.11 = (bf16[768,768]{1,0:T(8,128)(2,1)S(1)}, bf16[768,768]{1,0:T(8,128)(2,1)}, u32[]{:S(2)}) copy-start(bf16[768,768]{1,0:T(8,128)(2,1)} %copy-done.10) | copy-start | bytes 3538948
  153.1 2.1 %copy-start.13 = (bf16[768,256]{1,0:T(8,128)(2,1)S(1)}, bf16[768,256]{1,0:T(8,128)(2,1)}, u32[]{:S(2)}) copy-start(bf16[768,256]{1,0:T(8,128)(2,1)} %copy-done.12) | copy-start | bytes 1179652
  153.4 14.6 %collective-permute-start.24 = (bf16[64,4096]{1,0:T(8,128)(2,1)S(1)}, bf16[64,4096]{1,0:T(8,128)(2,1)S(1)}, u32[]{:S(2)}, u32[]{:S(2)}) collective-permute-start(bf16[64,4096]{1,0:T(8,128)(2,1)S(1)} %slice.209), channel_id=1, source_target_pairs={{0,2},{1,3},{4,6},{5,7},{8,10},{9,11},{12,14},{13,15},{2,0},{3,1},... | collective-permute-start | bytes 1572872 | tf_op jit(solution)/shard_map/ppermute | solution.py:38
  155.2 14.5 %collective-permute-start.25 = (bf16[64,4096]{1,0:T(8,128)(2,1)S(1)}, bf16[64,4096]{1,0:T(8,128)(2,1)S(1)}, u32[]{:S(2)}, u32[]{:S(2)}) collective-permute-start(bf16[64,4096]{1,0:T(8,128)(2,1)S(1)} %add_convert_fusion.3), channel_id=1, source_target_pairs={{0,8},{1,9},{4,12},{5,13},{8,0},{9,1},{12,4},{13,5},{2,10},{3,11},... | collective-permute-start | bytes 1572872 | tf_op jit(solution)/shard_map/ppermute | solution.py:38
  155.2 17.0 %copy-start.19 = (bf16[256,4096]{1,0:T(8,128)(2,1)S(1)}, bf16[256,4096]{1,0:T(8,128)(2,1)}, u32[]{:S(2)}) copy-start(bf16[256,4096]{1,0:T(8,128)(2,1)} %copy-done.17) | copy-start | bytes 6291460
  169.8 15.2 %copy-start.34 = (s32[64]{0:T(128)S(1)}, s32[64]{0:T(128)}, u32[]{:S(2)}) copy-start(s32[64]{0:T(128)} %copy-done.33) | copy-start | bytes 772
  169.9 15.2 %copy-start.36 = (s32[256]{0:T(256)S(1)}, s32[256]{0:T(256)}, u32[]{:S(2)}) copy-start(s32[256]{0:T(256)} %copy-done.35) | copy-start | bytes 3076
  169.9 15.2 %collective-permute-start.26 = (bf16[64,4096]{1,0:T(8,128)(2,1)S(1)}, bf16[64,4096]{1,0:T(8,128)(2,1)S(1)}, u32[]{:S(2)}, u32[]{:S(2)}) collective-permute-start(bf16[64,4096]{1,0:T(8,128)(2,1)S(1)} %add_convert_fusion.2), channel_id=1, source_target_pairs={{16,0},{32,16},{48,32},{17,1},{33,17},{49,33},{18,2},{34,18},{50,3... | collective-permute-start | bytes 1572872 | tf_op jit(solution)/shard_map/ppermute | solution.py:322
  172.2 14.9 %copy-start.1 = (bf16[1,1,256,4096]{3,2,1,0:T(8,128)(2,1)S(1)}, bf16[1,1,256,4096]{3,2,1,0:T(8,128)(2,1)}, u32[]{:S(2)}) copy-start(bf16[1,1,256,4096]{3,2,1,0:T(8,128)(2,1)} %param.7) | copy-start | bytes 6291460
